TPU v7x, 32 devices: a whole 2x2x4 slice. The times are simulated.
32 devices in a mesh: coil: 4 (over y, x), slab: 8 (over z, core).
Axes of the slice: x: 2, y: 2, z: 4, core: 2. Of those that a mesh axis runs over, the one named last changes fastest.
Arguments:
- coil_maps: float32 [8, 2, 8, 256, 128], P('coil', None, 'slab'), may hold values from -1.5 to 1.5
- kspace: float32 [8, 2, 8, 256, 128], P('coil', None, 'slab'), may hold values from -6 to 6
- sample_mask: int32 [256, 128], replicated, may hold values 0 or 1
- iterate: float32 [2, 8, 256, 128], P(None, 'slab', 'coil'), may hold values from -6 to 6
- probe_bits: int32 [2, 8, 256, 128], P(None, 'slab', 'coil'), may hold values from 0 to 1
- loss_gradient: float32 [2, 8, 256, 128], P(None, 'slab', 'coil'), may hold values from -6 to 6
- adjoint: float32 [2, 8, 256, 128], P(None, 'slab', 'coil'), may hold values from -6 to 6
- kernel_first: bfloat16 [24, 2, 3, 3, 3], replicated, may hold values from -0.875 to 0.875
- kernel_second: bfloat16 [24, 24, 3, 3, 3], replicated, may hold values from -0.25 to 0.25
- kernel_last: bfloat16 [2, 24, 3, 3, 3], replicated, may hold values from -0.25 to 0.25
Outputs:
- new_iterate: float32 [2, 8, 256, 128], P(None, 'slab', 'coil')
- probe_pullback: float32 [2, 8, 256, 128], P(None, 'slab', 'coil')
- adjoint_next: float32 [2, 8, 256, 128], P(None, 'slab', 'coil')
Inputs may be any that keep to these rules, and one draw needn't show every extreme that they name: `sample_mask`: 1 marks a sampled phase-encode line. `probe_bits`: the probe's sign is 2 p - 1.
All inputs are finite; a program needn't handle non-finite values.
Results may differ from a plain program's by a relative error of at most 0.0055.
Values may be sent and summed in bfloat16 or wider, within the bound.
A program may use at most 128 MiB of HBM per device.

v0:
```python
import math

import jax
import jax.numpy as jnp
from jax import lax
from jax.sharding import PartitionSpec as P

step_size = 0.8
kernel_layout = ("NCDHW", "OIDHW", "NCDHW")


def with_halo(cells, sides, width):
    for axis, dim in sides:
        count = lax.axis_size(axis)
        ends = count - 1
        head = lax.slice_in_dim(cells, 0, width, axis=dim)
        tail = lax.slice_in_dim(cells, cells.shape[dim] - width, cells.shape[dim], axis=dim)
        cells = jnp.concatenate(
            [
                lax.ppermute(tail, axis, [(i, (i + 1) % count) for i in range(ends)]),
                cells,
                lax.ppermute(head, axis, [((i + 1) % count, i) for i in range(ends)]),
            ],
            axis=dim,
        )
    return cells


def fourier_table(length, inverse):
    counter = jnp.arange(length, dtype=jnp.int32)
    phase_index = counter[:, None] * counter[None, :] % length
    angles = phase_index.astype(jnp.float32) * (2.0 * math.pi / length)
    norm_scale = 1.0 / math.sqrt(length)
    sine_sign = 1.0 if inverse else -1.0
    return (jnp.cos(angles) * norm_scale, sine_sign * jnp.sin(angles) * norm_scale)


def spectrum(real_part, imag_part, tables):
    height_cos, height_sin, depth_cos, depth_sin = tables
    highest = lax.Precision.HIGHEST
    along_real = jnp.einsum("...z,zw->...w", real_part, depth_cos, precision=highest) - jnp.einsum(
        "...z,zw->...w", imag_part, depth_sin, precision=highest
    )
    along_imag = jnp.einsum("...z,zw->...w", real_part, depth_sin, precision=highest) + jnp.einsum(
        "...z,zw->...w", imag_part, depth_cos, precision=highest
    )
    final_real = jnp.einsum(
        "yv,...vz->...yz", height_cos, along_real, precision=highest
    ) - jnp.einsum("yv,...vz->...yz", height_sin, along_imag, precision=highest)
    final_imag = jnp.einsum(
        "yv,...vz->...yz", height_sin, along_real, precision=highest
    ) + jnp.einsum("yv,...vz->...yz", height_cos, along_imag, precision=highest)
    return (final_real, final_imag)


def coil_partial(field, coil_maps, kspace, mask_weight, forward_tables, inverse_tables, with_data):
    field_real = field[:, 0]
    field_imag = field[:, 1]
    running = jnp.zeros(field.shape, jnp.float32)
    for coil_index in range(coil_maps.shape[0]):
        map_real = coil_maps[coil_index, 0]
        map_imag = coil_maps[coil_index, 1]
        coil_real = map_real * field_real - map_imag * field_imag
        coil_imag = map_real * field_imag + map_imag * field_real
        freq_real, freq_imag = spectrum(coil_real, coil_imag, forward_tables)
        freq_real = mask_weight * freq_real
        freq_imag = mask_weight * freq_imag
        if with_data:
            freq_real = freq_real - mask_weight * kspace[coil_index, 0]
            freq_imag = freq_imag - mask_weight * kspace[coil_index, 1]
        back_real, back_imag = spectrum(freq_real, freq_imag, inverse_tables)
        running = running + jnp.stack(
            [
                map_real * back_real + map_imag * back_imag,
                map_real * back_imag - map_imag * back_real,
            ],
            axis=1,
        )
    return running


def convolve_local(haloed, kernel):
    return lax.conv_general_dilated(
        haloed,
        kernel,
        (1, 1, 1),
        ((0, 0), (0, 0), (1, 1)),
        dimension_numbers=kernel_layout,
        preferred_element_type=jnp.float32,
    )


def transposed(kernel):
    return jnp.swapaxes(jnp.flip(kernel, (2, 3, 4)), 0, 1)


def silu_slope(preact):
    sigmoid_value = jax.nn.sigmoid(preact)
    return sigmoid_value * (1.0 + preact * (1.0 - sigmoid_value))


def feature_border(values):
    return with_halo(values, (("coil", 3), ("slab", 2)), 1)


def border_paired(values):
    return with_halo(values, (("coil", 3), ("slab", 2)), 1)


def on_device(
    coil_maps,
    kspace,
    sample_mask,
    iterate,
    probe_bits,
    loss_gradient,
    adjoint,
    kernel_first,
    kernel_second,
    kernel_last,
):
    height = sample_mask.shape[0]
    depth = sample_mask.shape[1]
    forward_tables = fourier_table(height, False) + fourier_table(depth, False)
    inverse_tables = fourier_table(height, True) + fourier_table(depth, True)
    mask_weight = sample_mask.astype(jnp.float32)
    row_count = iterate.shape[2]
    gathered = lax.all_gather(iterate.astype(jnp.bfloat16), "coil", axis=2, tiled=True).astype(
        iterate.dtype
    )
    partial_sum = coil_partial(
        gathered[None], coil_maps, kspace, mask_weight, forward_tables, inverse_tables, True
    )[0]
    summed = lax.psum(partial_sum, "coil")
    my_share = lax.dynamic_slice_in_dim(summed, lax.axis_index("coil") * row_count, row_count, 2)
    relaxed = iterate - step_size * my_share
    activation = relaxed.astype(jnp.bfloat16)[None]
    preacts = []
    for kernel in (kernel_first, kernel_second):
        preact = convolve_local(feature_border(activation), kernel)
        preacts.append(preact)
        activation = jax.nn.silu(preact).astype(jnp.bfloat16)
    new_iterate = relaxed + convolve_local(feature_border(activation), kernel_last)[0]
    sign_field = (2 * probe_bits - 1).astype(jnp.float32)
    cotangent = jnp.stack([sign_field, adjoint])
    grad_field = convolve_local(
        border_paired(cotangent.astype(jnp.bfloat16)), transposed(kernel_last)
    )
    for kernel, preact in ((kernel_second, preacts[1]), (kernel_first, preacts[0])):
        grad_field = (grad_field * silu_slope(preact)).astype(jnp.bfloat16)
        grad_field = convolve_local(border_paired(grad_field), transposed(kernel))
    pulled = cotangent + grad_field
    spread = lax.all_gather(pulled.astype(jnp.bfloat16), "coil", axis=3, tiled=True).astype(
        pulled.dtype
    )
    back_partial = coil_partial(
        spread, coil_maps, kspace, mask_weight, forward_tables, inverse_tables, False
    )
    back_summed = lax.psum(back_partial.astype(jnp.bfloat16), "coil").astype(jnp.float32)
    back_share = lax.dynamic_slice_in_dim(
        back_summed, lax.axis_index("coil") * row_count, row_count, 3
    )
    result = pulled - step_size * back_share
    return (new_iterate, result[0], loss_gradient + result[1])


def solution(mesh):
    in_specs = (
        P("coil", None, "slab", None, None),
        P("coil", None, "slab", None, None),
        P(),
        P(None, "slab", "coil", None),
        P(None, "slab", "coil", None),
        P(None, "slab", "coil", None),
        P(None, "slab", "coil", None),
        P(),
        P(),
        P(),
    )
    out_specs = (
        P(None, "slab", "coil", None),
        P(None, "slab", "coil", None),
        P(None, "slab", "coil", None),
    )
    return jax.shard_map(
        on_device, mesh=mesh, in_specs=in_specs, out_specs=out_specs, check_vma=False
    )
```

profile of v0, /device:TPU:0, one launch (start us, length us, event | category | flops | bytes accessed | tf_op | source)
XLA Modules:
  0.0 784.5 jit_solution(2926396361653520930)
XLA Ops:
  7.2 2.0 slice_bitcast_fusion.11
  10.2 9.9 %all_gather.6 = bf16[2,1,256,128]{3,0,1,2:T(2,128)(2,1)S(1)} all-gather(bf16[2,1,64,128]{3,0,1,2:T(2,128)(2,1)S(1)} %copy.561), channel_id=1, replica_groups=mesh['coil'=4,'slab'=8] {'coil'}, dimensions={2}, use_global_device_ids=true | all-gather | bytes 163840 | tf_op jit(solution)/shard_map/all_gather | solution.py:128
  56.2 4.6 collective-permute-start.12
  60.9 2.0 collective-permute-done.13
  64.7 3.0 collective-permute-start.14
  67.8 30.6 %all-reduce.3.cloned.1.call-done = f32[2,1,256,128]{2,3,1,0:T(8,128)} async-done(((f32[2,1,256,128]{2,3,1,0:T(8,128)}), f32[2,1,256,128]{2,3,1,0:T(8,128)}) %all-reduce.3.cloned.1.call-update) | async-done | bytes 262160 | tf_op jit(solution)/shard_map/psum | solution.py:134
  100.8 4.5 collective-permute-start
  108.6 3.2 collective-permute-start.2
  112.4 3.5 copy.419
  116.5 2.0 copy.388
  118.7 9.5 %fusion.31 = f32[1,64,8,17,24]{4,2,3,1,0:T(8,128)} fusion(bf16[24,2,3,3,3]{0,1,4,3,2:T(2,128)(2,1)S(1)} %copy-done.35, bf16[2,3,66,1,7,2]{4,0,5,2,1,3:T(2,128)(2,1)S(1)} %slice.134, bf16[2,3,66,1,8,17]{4,0,5,2,1,3:T(2,128)(2,1)S(1)} %copy.388), kind=kOutput, calls=%fused_computation.38 | convolution fusion | flops 22921920 | bytes 956976 | tf_op jit(solution)/shard_map/conv_general_dilated | solution.py:83
  128.2 4.0 copy.389
  132.2 1.9 add_multiply_fusion.1
  136.9 4.9 collective-permute-start.4
  147.0 4.0 collective-permute-start.6
  151.0 11.6 %broadcast_select_fusion.1 = f32[1,64,16,17,24]{4,2,3,1,0:T(8,128)} fusion(pred[16,17]{0,1:T(8,128)(4,1)S(1)} %copy-done.40, bf16[2,3,66,16,19]{3,0,4,2,1:T(2,128)(2,1)} %copy.419, bf16[2,24,3,3,3]{1,0,4,3,2:T(2,128)(2,1)S(1)} %copy-done.37), kind=kOutput, calls=%fused_computation.25 | convolution fusion | flops 45539328 | bytes 1914800 | tf_op jit(solution)/shard_map/conv_general_dilated | solution.py:83
  162.6 8.8 %copy.420 = f32[1,64,16,17,24]{1,4,3,2,0:T(8,128)} copy(f32[1,64,16,17,24]{4,2,3,1,0:T(8,128)} %broadcast_select_fusion.1) | data formatting | bytes 3342336 | tf_op jit(solution)/shard_map/conv_general_dilated | solution.py:83
  172.9 2.4 copy.397
  175.3 2.6 maximum_bitcast_fusion.2
  178.4 8.2 %copy.400 = bf16[24,3,66,1,8,17]{0,4,5,2,1,3:T(8,128)(2,1)} copy(bf16[24,3,66,1,8,17]{2,0,5,4,1,3:T(8,128)(2,1)S(1)} %bitcast.484) | data formatting | bytes 2585088 | tf_op jit(solution)/shard_map/conv_general_dilated | solution.py:83
  187.9 12.9 %fusion.10 = f32[1,64,8,17,24]{4,2,3,1,0:T(8,128)} fusion(bf16[24,24,3,3,3]{1,0,4,3,2:T(8,128)(2,1)S(1)} %copy-done, bf16[24,3,66,1,7,2]{0,4,5,2,1,3:T(8,128)(2,1)S(1)} %slice.140, bf16[24,3,66,1,8,17]{0,4,5,2,1,3:T(8,128)(2,1)} %copy.400), kind=kOutput, calls=%fused_computation.12 | convolution fusion | flops 275063040 | bytes 2292288 | tf_op jit(solution)/shard_map/conv_general_dilated | solution.py:83
  200.8 4.0 copy.401
  207.3 1.9 fusion.598
  209.2 2.2 copy.422
  213.7 5.8 collective-permute-start.16
  222.6 4.0 pad_maximum_fusion
  226.6 3.1 copy.425
  230.9 4.0 collective-permute-start.18
  234.9 2.7 slice_bitcast_fusion.2
  237.6 2.9 copy.428
  240.5 2.8 copy.427
  243.3 4.8 maximum_bitcast_fusion
  249.1 3.3 fusion.19
  252.4 26.3 %copy.429 = bf16[24,3,66,2,8,19]{0,4,3,5,2,1:T(8,128)(2,1)} copy(bf16[24,3,66,2,8,19]{2,0,5,4,3,1:T(8,128)(2,1)} %fusion.19) | data formatting | bytes 5778432 | tf_op jit(solution)/shard_map/conv_general_dilated | solution.py:83
  278.7 23.4 %broadcast_select_fusion = f32[1,64,16,17,24]{4,2,3,1,0:T(8,128)} fusion(pred[16,17]{0,1:T(8,128)(4,1)S(1)} %copy-done.40, bf16[24,24,3,3,3]{1,0,4,3,2:T(8,128)(2,1)S(1)} %copy-done, bf16[24,3,66,2,8,19]{0,4,3,5,2,1:T(8,128)(2,1)} %copy.429), kind=kOutput, calls=%fused_computation.24 | convolution fusion | flops 541876224 | bytes 4591760 | tf_op jit(solution)/shard_map/conv_general_dilated | solution.py:83
  302.2 8.9 %copy.430 = f32[1,64,16,17,24]{1,4,3,2,0:T(8,128)} copy(f32[1,64,16,17,24]{4,2,3,1,0:T(8,128)} %broadcast_select_fusion) | data formatting | bytes 3342336 | tf_op jit(solution)/shard_map/conv_general_dilated | solution.py:83
  311.1 2.3 fusion.26
  313.4 2.3 fusion.597
  315.8 2.2 copy.432
  319.3 2.6 copy.431
  321.9 5.7 collective-permute-start.20
  330.4 5.7 collective-permute-start.8
  338.9 4.0 pad_maximum_fusion.1
  342.9 3.1 copy.435
  347.3 8.2 %collective-permute-start.22 = (bf16[2,24,1,66,128]{4,1,3,2,0:T(8,128)(2,1)}, bf16[2,24,1,66,128]{4,1,3,2,0:T(8,128)(2,1)}, u32[]{:S(2)}, u32[]{:S(2)}) collective-permute-start(bf16[2,24,1,66,128]{4,1,3,2,0:T(8,128)(2,1)} %copy.435), channel_id=1, source_target_pairs={{0,1},{1,2},{2,3},{3,4},{4,5},{5,6},{6,7},{8,9},{9,10},{10,11},{11... | collective-permute-start | bytes 2433032 | tf_op jit(solution)/shard_map/ppermute | solution.py:20
  355.5 2.1 slice_bitcast_fusion.4
  360.2 3.2 pad_maximum_fusion.3
  363.4 2.5 copy.407
  367.2 4.1 collective-permute-start.10
  372.1 2.4 copy.410
  374.5 2.4 copy.409
  376.9 3.0 maximum_bitcast_fusion.3
  379.9 1.9 pad.4
  381.8 9.8 %copy.412 = bf16[24,3,66,1,8,17]{0,4,5,2,1,3:T(8,128)(2,1)} copy(bf16[24,3,66,1,8,17]{2,0,5,4,1,3:T(8,128)(2,1)} %bitcast.485) | data formatting | bytes 2585088 | tf_op jit(solution)/shard_map/conv_general_dilated | solution.py:83
  391.6 2.3 slice.146
  393.9 2.8 copy.438
  396.7 2.9 copy.437
  399.6 4.8 maximum_bitcast_fusion.1
  405.4 3.3 fusion.20
  408.6 26.3 %copy.439 = bf16[24,3,66,2,8,19]{0,4,3,5,2,1:T(8,128)(2,1)} copy(bf16[24,3,66,2,8,19]{2,0,5,4,3,1:T(8,128)(2,1)} %fusion.20) | data formatting | bytes 5778432 | tf_op jit(solution)/shard_map/conv_general_dilated | solution.py:83
  435.0 147.3 %broadcast_select_fusion.2 = f32[1,64,16,17,2]{2,4,3,1,0:T(2,128)S(1)} fusion(pred[16,17]{0,1:T(8,128)(4,1)S(1)} %copy-done.40, bf16[24,2,3,3,3]{0,1,4,3,2:T(2,128)(2,1)S(1)} %copy-done.36, bf16[24,3,66,2,8,19]{0,4,3,5,2,1:T(8,128)(2,1)} %copy.439), kind=kOutput, calls=%fused_computation.119 | convolution fusion | flops 45156352 | bytes 3031344 | tf_op jit(solution)/shard_map/conv_general_dilated | solution.py:83
  583.6 10.5 %all_gather.7 = bf16[2,2,1,256,128]{4,1,2,0,3:T(2,128)(2,1)S(1)} all-gather(bf16[2,2,1,64,128]{4,1,2,0,3:T(2,128)(2,1)S(1)} %copy.443), channel_id=1, replica_groups=mesh['coil'=4,'slab'=8] {'coil'}, dimensions={3}, use_global_device_ids=true | all-gather | bytes 327680 | tf_op jit(solution)/shard_map/all_gather | solution.py:153
  605.5 1.9 fusion.81
  631.2 142.0 %fusion.69 = f32[1,64,8,17,2]{2,4,3,1,0:T(2,128)S(1)} fusion(bf16[2,24,3,3,3]{1,0,4,3,2:T(2,128)(2,1)S(1)} %copy-done.38, bf16[24,3,66,1,7,2]{0,4,5,2,1,3:T(8,128)(2,1)S(1)} %copy-done.19, bf16[24,3,66,1,8,17]{0,4,5,2,1,3:T(8,128)(2,1)} %copy.412, pred[8,17]{0,1:T(8,128)(4,1)S(1)} %copy-done.39), kind=kOutput, calls=%fused_computation.118 | convolution fusion | flops 26912000 | bytes 1497960 | tf_op jit(solution)/shard_map/conv_general_dilated | solution.py:83
  (274 shorter events, 120.8 us)
Async XLA Ops:
  7.2 180.7 %copy-start = (bf16[24,24,3,3,3]{1,0,4,3,2:T(8,128)(2,1)S(1)}, bf16[24,24,3,3,3]{1,0,4,3,2:T(8,128)(2,1)}, u32[]{:S(2)}) copy-start(bf16[24,24,3,3,3]{1,0,4,3,2:T(8,128)(2,1)} %param.18) | copy-start | bytes 93316
  7.2 91.2 %all-reduce.3.cloned.1.call-start = ((), (), s32[]{:S(2)}) async-start(), calls=%async_computation | async-start | bytes 524288 | tf_op jit(solution)/shard_map/psum | solution.py:134
  9.3 39.6 %copy-start.9 = (f32[1,1,1,256,128]{3,4,2,1,0:T(8,128)}, f32[1,1,1,256,128]{3,4,2,1,0:T(8,128)S(1)}, u32[]{:S(2)}) copy-start(f32[1,1,1,256,128]{3,4,2,1,0:T(8,128)S(1)} %copy.513) | copy-start | bytes 393220
  20.2 5.5 copy-start.24
  20.4 31.2 %copy-start.11 = (f32[1,1,1,256,128]{3,4,2,1,0:T(8,128)}, f32[1,1,1,256,128]{3,4,2,1,0:T(8,128)S(1)}, u32[]{:S(2)}) copy-start(f32[1,1,1,256,128]{3,4,2,1,0:T(8,128)S(1)} %copy.517) | copy-start | bytes 393220
  20.5 31.1 %copy-start.13 = (f32[1,1,1,256,128]{3,4,2,1,0:T(8,128)}, f32[1,1,1,256,128]{3,4,2,1,0:T(8,128)S(1)}, u32[]{:S(2)}) copy-start(f32[1,1,1,256,128]{3,4,2,1,0:T(8,128)S(1)} %copy.516) | copy-start | bytes 393220
  20.7 28.2 %copy-start.15 = (f32[1,1,1,256,128]{3,4,2,1,0:T(8,128)}, f32[1,1,1,256,128]{3,4,2,1,0:T(8,128)S(1)}, u32[]{:S(2)}) copy-start(f32[1,1,1,256,128]{3,4,2,1,0:T(8,128)S(1)} %copy.512) | copy-start | bytes 393220
  20.7 5.2 copy-start.29
  26.0 15.2 %copy-start.25 = (s32[256,128]{0,1:T(8,128)}, s32[256,128]{0,1:T(8,128)S(1)}, u32[]{:S(2)}) copy-start(s32[256,128]{0,1:T(8,128)S(1)} %copy.374) | copy-start | bytes 393220
  47.5 6.4 copy-start.31
  47.5 6.5 copy-start.32
  48.9 11.9 %copy-start.28 = (f32[2,1,64,128]{3,2,1,0:T(8,128)S(1)}, f32[2,1,64,128]{3,2,1,0:T(8,128)}, u32[]{:S(2)}) copy-start(f32[2,1,64,128]{3,2,1,0:T(8,128)} %param.13) | copy-start | bytes 196612
  53.8 721.3 %all-reduce.5.cloned.1.call-start = ((), (), s32[]{:S(2)}) async-start(), calls=%async_computation.1 | async-start | bytes 524288 | tf_op jit(solution)/shard_map/psum | solution.py:159
  54.0 58.3 %copy-start.5 = (f32[2,1,64,128]{2,3,0,1:T(8,128)}, f32[2,1,64,128]{2,3,0,1:T(8,128)S(1)}, u32[]{:S(2)}) copy-start(f32[2,1,64,128]{2,3,0,1:T(8,128)S(1)} %copy.416) | copy-start | bytes 196612
  54.9 8.0 %collective-permute-start.13 = (bf16[2,2,1,1,128]{3,4,0,2,1:T(8,128)(2,1)S(1)}, bf16[2,2,1,1,128]{3,4,0,2,1:T(8,128)(2,1)S(1)}, u32[]{:S(2)}, u32[]{:S(2)}) collective-permute-start(bf16[2,2,1,1,128]{3,4,0,2,1:T(8,128)(2,1)S(1)} %get-tuple-element.65), channel_id=1, source_target_pairs={{8,0},{16,8},{24,16},{9,1},{17,9},{25,17},{10,2},{18,10},{26,18},{... | collective-permute-start | bytes 3080 | tf_op jit(solution)/shard_map/ppermute | solution.py:22
  56.2 7.1 collective-permute-start.12
  60.9 44.4 %copy-start.17 = (f32[2,1,64,128]{2,3,1,0:T(8,128)}, f32[2,1,64,128]{2,3,1,0:T(8,128)S(1)}, u32[]{:S(2)}) copy-start(f32[2,1,64,128]{2,3,1,0:T(8,128)S(1)} %copy.384) | copy-start | bytes 196612
  63.4 41.9 %collective-permute-start.15 = (bf16[2,2,1,66,128]{3,4,0,2,1:T(8,128)(2,1)S(1)}, bf16[2,2,1,66,128]{3,4,0,2,1:T(8,128)(2,1)S(1)}, u32[]{:S(2)}, u32[]{:S(2)}) collective-permute-start(bf16[2,2,1,66,128]{3,4,0,2,1:T(8,128)(2,1)S(1)} %pad_maximum_fusion.5), channel_id=1, source_target_pairs={{1,0},{2,1},{3,2},{4,3},{5,4},{6,5},{7,6},{9,8},{10,9},{11,10},{12... | collective-permute-start | bytes 202760 | tf_op jit(solution)/shard_map/ppermute | solution.py:22
  64.7 40.6 %collective-permute-start.14 = (bf16[2,2,1,66,128]{3,4,0,2,1:T(8,128)(2,1)S(1)}, bf16[2,2,1,66,128]{3,4,0,2,1:T(8,128)(2,1)S(1)}, u32[]{:S(2)}, u32[]{:S(2)}) collective-permute-start(bf16[2,2,1,66,128]{3,4,0,2,1:T(8,128)(2,1)S(1)} %pad_maximum_fusion.5), channel_id=1, source_target_pairs={{0,1},{1,2},{2,3},{3,4},{4,5},{5,6},{6,7},{8,9},{9,10},{10,11},{11... | collective-permute-start | bytes 202760 | tf_op jit(solution)/shard_map/ppermute | solution.py:20
  99.5 6.9 collective-permute-start.1
  100.8 6.4 collective-permute-start
  107.3 8.6 %collective-permute-start.3 = (bf16[1,2,1,66,128]{3,4,1,2,0:T(8,128)(2,1)S(1)}, bf16[1,2,1,66,128]{3,4,1,2,0:T(8,128)(2,1)S(1)}, u32[]{:S(2)}, u32[]{:S(2)}) collective-permute-start(bf16[1,2,1,66,128]{3,4,1,2,0:T(8,128)(2,1)S(1)} %pad_maximum_fusion.6), channel_id=1, source_target_pairs={{1,0},{2,1},{3,2},{4,3},{5,4},{6,5},{7,6},{9,8},{10,9},{11,10},{12... | collective-permute-start | bytes 101384 | tf_op jit(solution)/shard_map/ppermute | solution.py:22
  108.6 7.3 collective-permute-start.2
  112.4 6.3 copy-start.35
  135.5 6.5 collective-permute-start.5
  136.9 6.3 collective-permute-start.4
  141.9 9.0 %copy-start.37 = (bf16[2,24,3,3,3]{1,0,4,3,2:T(2,128)(2,1)S(1)}, bf16[2,24,3,3,3]{1,0,4,3,2:T(2,128)(2,1)}, u32[]{:S(2)}) copy-start(bf16[2,24,3,3,3]{1,0,4,3,2:T(2,128)(2,1)} %param.19) | copy-start | bytes 7780
  141.9 9.0 %copy-start.40 = (pred[16,17]{0,1:T(8,128)(4,1)S(1)}, pred[16,17]{0,1:T(8,128)(4,1)}, u32[]{:S(2)}) copy-start(pred[16,17]{0,1:T(8,128)(4,1)} %constant.103) | copy-start | bytes 820
  145.7 25.7 %collective-permute-start.7 = (bf16[1,24,1,66,128]{4,1,3,2,0:T(8,128)(2,1)}, bf16[1,24,1,66,128]{4,1,3,2,0:T(8,128)(2,1)}, u32[]{:S(2)}, u32[]{:S(2)}) collective-permute-start(bf16[1,24,1,66,128]{4,1,3,2,0:T(8,128)(2,1)} %copy.395), channel_id=1, source_target_pairs={{1,0},{2,1},{3,2},{4,3},{5,4},{6,5},{7,6},{9,8},{10,9},{11,10},{12... | collective-permute-start | bytes 1216520 | tf_op jit(solution)/shard_map/ppermute | solution.py:22
  147.0 25.9 %collective-permute-start.6 = (bf16[1,24,1,66,128]{4,1,3,2,0:T(8,128)(2,1)}, bf16[1,24,1,66,128]{4,1,3,2,0:T(8,128)(2,1)}, u32[]{:S(2)}, u32[]{:S(2)}) collective-permute-start(bf16[1,24,1,66,128]{4,1,3,2,0:T(8,128)(2,1)} %copy.395), channel_id=1, source_target_pairs={{0,1},{1,2},{2,3},{3,4},{4,5},{5,6},{6,7},{8,9},{9,10},{10,11},{11... | collective-permute-start | bytes 1216520 | tf_op jit(solution)/shard_map/ppermute | solution.py:20
  211.4 8.1 %collective-permute-start.17 = (bf16[2,24,1,1,128]{4,1,3,2,0:T(8,128)(2,1)S(1)}, bf16[2,24,1,1,128]{4,1,3,2,0:T(8,128)(2,1)S(1)}, u32[]{:S(2)}, u32[]{:S(2)}) collective-permute-start(bf16[2,24,1,1,128]{4,1,3,2,0:T(8,128)(2,1)S(1)} %copy.422), channel_id=1, source_target_pairs={{8,0},{16,8},{24,16},{9,1},{17,9},{25,17},{10,2},{18,10},{26,18},{... | collective-permute-start | bytes 36872 | tf_op jit(solution)/shard_map/ppermute | solution.py:22
  213.7 7.2 collective-permute-start.16
  229.6 8.0 %collective-permute-start.19 = (bf16[2,24,1,66,128]{4,1,3,2,0:T(8,128)(2,1)}, bf16[2,24,1,66,128]{4,1,3,2,0:T(8,128)(2,1)}, u32[]{:S(2)}, u32[]{:S(2)}) collective-permute-start(bf16[2,24,1,66,128]{4,1,3,2,0:T(8,128)(2,1)} %copy.425), channel_id=1, source_target_pairs={{1,0},{2,1},{3,2},{4,3},{5,4},{6,5},{7,6},{9,8},{10,9},{11,10},{12... | collective-permute-start | bytes 2433032 | tf_op jit(solution)/shard_map/ppermute | solution.py:22
  230.9 9.6 %collective-permute-start.18 = (bf16[2,24,1,66,128]{4,1,3,2,0:T(8,128)(2,1)}, bf16[2,24,1,66,128]{4,1,3,2,0:T(8,128)(2,1)}, u32[]{:S(2)}, u32[]{:S(2)}) collective-permute-start(bf16[2,24,1,66,128]{4,1,3,2,0:T(8,128)(2,1)} %copy.425), channel_id=1, source_target_pairs={{0,1},{1,2},{2,3},{3,4},{4,5},{5,6},{6,7},{8,9},{9,10},{10,11},{11... | collective-permute-start | bytes 2433032 | tf_op jit(solution)/shard_map/ppermute | solution.py:20
  302.2 8.9 %copy-start.4 = (f32[24,64,128]{1,0,2:T(8,128)S(1)}, f32[24,64,128]{1,0,2:T(8,128)}, u32[]{:S(2)}) copy-start(f32[24,64,128]{1,0,2:T(8,128)} %slice_bitcast_fusion.2) | copy-start | bytes 2359300
  315.8 11.9 %copy-start.2 = (bf16[1,64,8,17,24]{1,4,3,2,0:T(8,128)(2,1)S(1)}, bf16[1,64,8,17,24]{1,4,3,2,0:T(8,128)(2,1)}, u32[]{:S(2)}) copy-start(bf16[1,64,8,17,24]{1,4,3,2,0:T(8,128)(2,1)} %get-tuple-element.25) | copy-start | bytes 1253380
  318.0 18.1 %collective-permute-start.21 = (bf16[2,24,1,1,128]{4,1,3,2,0:T(8,128)(2,1)S(1)}, bf16[2,24,1,1,128]{4,1,3,2,0:T(8,128)(2,1)S(1)}, u32[]{:S(2)}, u32[]{:S(2)}) collective-permute-start(bf16[2,24,1,1,128]{4,1,3,2,0:T(8,128)(2,1)S(1)} %copy.432), channel_id=1, source_target_pairs={{8,0},{16,8},{24,16},{9,1},{17,9},{25,17},{10,2},{18,10},{26,18},{... | collective-permute-start | bytes 36872 | tf_op jit(solution)/shard_map/ppermute | solution.py:22
  321.9 15.2 %collective-permute-start.20 = (bf16[2,24,1,1,128]{4,1,3,2,0:T(8,128)(2,1)S(1)}, bf16[2,24,1,1,128]{4,1,3,2,0:T(8,128)(2,1)S(1)}, u32[]{:S(2)}, u32[]{:S(2)}) collective-permute-start(bf16[2,24,1,1,128]{4,1,3,2,0:T(8,128)(2,1)S(1)} %copy.431), channel_id=1, source_target_pairs={{0,8},{8,16},{16,24},{1,9},{9,17},{17,25},{2,10},{10,18},{18,26},{... | collective-permute-start | bytes 36872 | tf_op jit(solution)/shard_map/ppermute | solution.py:20
  329.0 28.7 %collective-permute-start.9 = (bf16[1,24,1,1,128]{4,1,3,2,0:T(8,128)(2,1)S(1)}, bf16[1,24,1,1,128]{4,1,3,2,0:T(8,128)(2,1)S(1)}, u32[]{:S(2)}, u32[]{:S(2)}) collective-permute-start(bf16[1,24,1,1,128]{4,1,3,2,0:T(8,128)(2,1)S(1)} %bitcast.503), channel_id=1, source_target_pairs={{8,0},{16,8},{24,16},{9,1},{17,9},{25,17},{10,2},{18,10},{26,18},{... | collective-permute-start | bytes 18440 | tf_op jit(solution)/shard_map/ppermute | solution.py:22
  330.4 28.6 %collective-permute-start.8 = (bf16[1,24,1,1,128]{4,1,0,3,2:T(8,128)(2,1)S(1)}, bf16[1,24,1,1,128]{4,1,0,3,2:T(8,128)(2,1)S(1)}, u32[]{:S(2)}, u32[]{:S(2)}) collective-permute-start(bf16[1,24,1,1,128]{4,1,0,3,2:T(8,128)(2,1)S(1)} %bitcast.504), channel_id=1, source_target_pairs={{0,8},{8,16},{16,24},{1,9},{9,17},{17,25},{2,10},{10,18},{18,26},{... | collective-permute-start | bytes 18440 | tf_op jit(solution)/shard_map/ppermute | solution.py:20
  346.0 47.9 %collective-permute-start.23 = (bf16[2,24,1,66,128]{4,1,3,2,0:T(8,128)(2,1)}, bf16[2,24,1,66,128]{4,1,3,2,0:T(8,128)(2,1)}, u32[]{:S(2)}, u32[]{:S(2)}) collective-permute-start(bf16[2,24,1,66,128]{4,1,3,2,0:T(8,128)(2,1)} %copy.435), channel_id=1, source_target_pairs={{1,0},{2,1},{3,2},{4,3},{5,4},{6,5},{7,6},{9,8},{10,9},{11,10},{12... | collective-permute-start | bytes 2433032 | tf_op jit(solution)/shard_map/ppermute | solution.py:22
  347.3 49.5 %collective-permute-start.22 = (bf16[2,24,1,66,128]{4,1,3,2,0:T(8,128)(2,1)}, bf16[2,24,1,66,128]{4,1,3,2,0:T(8,128)(2,1)}, u32[]{:S(2)}, u32[]{:S(2)}) collective-permute-start(bf16[2,24,1,66,128]{4,1,3,2,0:T(8,128)(2,1)} %copy.435), channel_id=1, source_target_pairs={{0,1},{1,2},{2,3},{3,4},{4,5},{5,6},{6,7},{8,9},{9,10},{10,11},{11... | collective-permute-start | bytes 2433032 | tf_op jit(solution)/shard_map/ppermute | solution.py:20
  357.6 13.7 %copy-start.26 = (s32[256,128]{0,1:T(8,128)S(1)}, s32[256,128]{0,1:T(8,128)}, u32[]{:S(2)}) copy-start(s32[256,128]{0,1:T(8,128)} %copy-done.25) | copy-start | bytes 393220
  357.6 14.4 %copy-start.33 = (f32[2,1,64,128]{3,2,1,0:T(8,128)S(1)}, f32[2,1,64,128]{3,2,1,0:T(8,128)}, u32[]{:S(2)}) copy-start(f32[2,1,64,128]{3,2,1,0:T(8,128)} %param.15) | copy-start | bytes 196612
  365.9 6.2 collective-permute-start.11
  367.2 7.3 collective-permute-start.10
  408.6 26.3 %copy-start.36 = (bf16[24,2,3,3,3]{0,1,4,3,2:T(2,128)(2,1)S(1)}, bf16[24,2,3,3,3]{0,1,4,3,2:T(2,128)(2,1)}, u32[]{:S(2)}) copy-start(bf16[24,2,3,3,3]{0,1,4,3,2:T(2,128)(2,1)} %param.17) | copy-start | bytes 7780
  435.0 148.4 %copy-start.6 = (f32[2,1,64,128]{2,3,0,1:T(8,128)S(1)}, f32[2,1,64,128]{2,3,0,1:T(8,128)}, u32[]{:S(2)}) copy-start(f32[2,1,64,128]{2,3,0,1:T(8,128)} %copy-done.5) | copy-start | bytes 196612
  435.0 148.4 %copy-start.8 = (f32[1,2,1,64,128]{3,4,0,2,1:T(8,128)S(1)}, f32[1,2,1,64,128]{3,4,0,2,1:T(8,128)}, u32[]{:S(2)}) copy-start(f32[1,2,1,64,128]{3,4,0,2,1:T(8,128)} %copy-done.7) | copy-start | bytes 196612
  582.2 12.2 %copy-start.20 = (f32[256,128]{1,0:T(8,128)S(1)}, f32[256,128]{1,0:T(8,128)}, u32[]{:S(2)}) copy-start(f32[256,128]{1,0:T(8,128)} %get-tuple-element.40) | copy-start | bytes 393220
  582.2 12.2 %copy-start.21 = (f32[256,128]{1,0:T(8,128)S(1)}, f32[256,128]{1,0:T(8,128)}, u32[]{:S(2)}) copy-start(f32[256,128]{1,0:T(8,128)} %get-tuple-element.41) | copy-start | bytes 393220
  582.2 12.2 %copy-start.22 = (f32[256,128]{1,0:T(8,128)S(1)}, f32[256,128]{1,0:T(8,128)}, u32[]{:S(2)}) copy-start(f32[256,128]{1,0:T(8,128)} %get-tuple-element.42) | copy-start | bytes 393220
  582.3 12.2 %copy-start.23 = (f32[256,128]{1,0:T(8,128)S(1)}, f32[256,128]{1,0:T(8,128)}, u32[]{:S(2)}) copy-start(f32[256,128]{1,0:T(8,128)} %get-tuple-element.43) | copy-start | bytes 393220
  594.4 5.9 copy-start.30
  621.2 7.5 copy-start.10
  621.2 7.5 copy-start.12
  621.3 7.5 copy-start.14
  621.3 7.5 copy-start.16
  626.5 4.6 copy-start.19
  626.5 4.6 copy-start.38
  626.5 4.6 copy-start.39
  631.1 143.1 %copy-start.18 = (f32[2,1,64,128]{2,3,1,0:T(8,128)S(1)}, f32[2,1,64,128]{2,3,1,0:T(8,128)}, u32[]{:S(2)}) copy-start(f32[2,1,64,128]{2,3,1,0:T(8,128)} %copy-done.17) | copy-start | bytes 196612
  631.1 143.1 %copy-start.27 = (f32[2,1,256,128]{2,3,1,0:T(8,128)S(1)}, f32[2,1,256,128]{2,3,1,0:T(8,128)}, u32[]{:S(2)}) copy-start(f32[2,1,256,128]{2,3,1,0:T(8,128)} %all-reduce.3.cloned.1.call-done) | copy-start | bytes 786436
  631.1 146.4 %copy-start.1 = (bf16[24,24,3,3,3]{1,0,4,3,2:T(8,128)(2,1)S(1)}, bf16[24,24,3,3,3]{1,0,4,3,2:T(8,128)(2,1)}, u32[]{:S(2)}) copy-start(bf16[24,24,3,3,3]{1,0,4,3,2:T(8,128)(2,1)} %param.18) | copy-start | bytes 93316
  (3 other events, 6.9 us)
Sparse Core Ops, SparseCore 0:
  53.9 44.3 all-reduce.2
  631.2 47.5 all-reduce.4
where the time goes:
time: 798 us; the launch traced here: 785 us
  matrix products  413 us (52%)
  local copies, waits for them, and re-layouts  181 us (23%)
  starting transfers between devices  73.4 us (9%)
  other arithmetic  45.8 us (6%)
  waiting for transfers between devices  35 us (4%)
  blocking collectives  20.4 us (3%)
  between operations  16 us (2%)
    conv_general_dilated x6, matrix products, convolve_local(): lax.conv_general_dilated(haloed, kernel, (1, 1, 1), ((0, 0), (0, 0), (1,...  347 us
    conv_general_dilated x21, local copies, waits for them, and re-layouts, convolve_local(): lax.conv_general_dilated(haloed, kernel, (1, 1, 1), ((0, 0), (0, 0), (1,...  108 us
    ppermute x12, starting transfers between devices, with_halo(): lax.ppermute(tail, axis, [(i, (i + 1) % count) for i in range(ends)])  57.8 us
    psum x1, waiting for transfers between devices, on_device(): summed = lax.psum(partial_sum, 'coil')  30.6 us
    concatenate x12, other arithmetic, with_halo(): jnp.concatenate([lax.ppermute(tail, axis, [(i, (i + 1) % count) for i in...  27.7 us
  transfers between devices with their start and end apart: 26, of which 6 were waited for; matrix products, arithmetic and copies ran while one was open for 29% of the time, Pallas kernels for 0%

commit v1 on v0

v1 whole, which is shorter than its diff:
```python
import math

import jax
import jax.numpy as jnp
import numpy as np
from jax import lax
from jax.experimental import pallas as pl
from jax.experimental.pallas import tpu as pltpu
from jax.sharding import PartitionSpec as P

step_size = 0.8
reach = 4
both = ("coil", "slab")
f32 = jnp.float32
bf16 = jnp.bfloat16
vmem = pl.BlockSpec(memory_space=pltpu.VMEM)
MESH = pl.DeviceIdType.MESH


def exchange(items, collective_id):
    coils, slabs = lax.axis_size("coil"), lax.axis_size("slab")
    count = len(items)
    sizes = [math.prod(lax.axis_size(a) for a in axes) for _, axes, _ in items]
    outs = []
    for (array, _, how), size in zip(items, sizes):
        tail = array.shape if how == "all" else array.shape[1:]
        outs.append(jax.ShapeDtypeStruct((size,) + tail, array.dtype))
    widest = items[int(np.argmax(sizes))][1]

    def kernel(*refs):
        sources, targets = refs[:count], refs[count : 2 * count]
        send_sems, recv_sems = refs[2 * count : 3 * count], refs[3 * count :]
        my_coil, my_slab = lax.axis_index("coil"), lax.axis_index("slab")

        def place(axes, rank):
            if axes == both:
                return lax.div(rank, slabs), lax.rem(rank, slabs)
            return (rank, my_slab) if axes == ("coil",) else (my_coil, rank)

        def my_rank(axes):
            if axes == both:
                return my_coil * slabs + my_slab
            return my_coil if axes == ("coil",) else my_slab

        def row(item, rank):
            if items[item][2] == "all":
                return sources[item]
            if items[item][2] == "slab":
                return sources[item].at[place(items[item][1], rank)[1]]
            return sources[item].at[rank]

        barrier = pltpu.get_barrier_semaphore()
        reached = max(sizes)

        def greet(step, carry):
            rank = lax.rem(my_rank(widest) + step, reached)
            pl.semaphore_signal(barrier, inc=1, device_id=place(widest, rank), device_id_type=MESH)
            return carry

        lax.fori_loop(1, reached, greet, 0)
        pl.semaphore_wait(barrier, reached - 1)

        def copy(item, step):
            axes, size = items[item][1], sizes[item]
            mine = my_rank(axes)
            rank = lax.rem(mine + step, size)
            return pltpu.make_async_remote_copy(
                src_ref=row(item, rank),
                dst_ref=targets[item].at[mine],
                send_sem=send_sems[item].at[step],
                recv_sem=recv_sems[item].at[step],
                device_id=place(axes, rank),
                device_id_type=MESH,
            )

        for item in range(count):
            lax.fori_loop(1, sizes[item], lambda s, c, item=item: (copy(item, s).start(), c)[1], 0)
        for item in range(count):
            mine = my_rank(items[item][1])
            targets[item][mine] = row(item, mine)[...]
        for item in range(count):
            axes, size = items[item][1], sizes[item]

            def finish(step, carry, item=item, axes=axes, size=size):
                mine = my_rank(axes)
                rank = lax.rem(mine + size - step, size)
                pltpu.make_async_remote_copy(
                    src_ref=row(item, mine),
                    dst_ref=targets[item].at[rank],
                    send_sem=send_sems[item].at[step],
                    recv_sem=recv_sems[item].at[step],
                    device_id=place(axes, rank),
                    device_id_type=MESH,
                ).wait()
                return carry

            lax.fori_loop(1, size, finish, 0)

    return pl.pallas_call(
        kernel,
        out_shape=outs,
        in_specs=[vmem] * count,
        out_specs=[vmem] * count,
        scratch_shapes=[pltpu.SemaphoreType.DMA((size,)) for size in sizes] * 2,
        compiler_params=pltpu.CompilerParams(collective_id=collective_id, has_side_effects=True),
    )(*[array for array, _, _ in items])


def split(table):
    high = jnp.asarray(table, f32).astype(bf16)
    return high, (jnp.asarray(table, f32) - high.astype(f32)).astype(bf16)


def fourier_tables(height, depth, sign):
    def parts(length):
        counter = np.arange(length)
        angles = (counter[:, None] * counter[None, :] % length) * (2.0 * np.pi / length)
        return np.cos(angles) / np.sqrt(length), sign * np.sin(angles) / np.sqrt(length)

    depth_cos, depth_sin = parts(depth)
    height_cos, height_sin = parts(height)
    along = np.block([[depth_cos, depth_sin], [-depth_sin, depth_cos]])
    down = np.concatenate([height_cos, height_sin], axis=0)
    return split(along) + split(down)


def dot(left, right):
    return jnp.dot(left, right, preferred_element_type=f32)


def halves(values):
    high = values.astype(bf16)
    return high, (values - high.astype(f32)).astype(bf16)


def spectrum(values, tables):
    along_high, along_low, down_high, down_low = tables
    height, depth = values.shape[0], values.shape[1] // 2
    high, low = halves(values)
    high, low = halves(
        dot(high, along_high[...]) + (dot(low, along_high[...]) + dot(high, along_low[...]))
    )
    both_parts = dot(down_high[...], high) + (dot(down_high[...], low) + dot(down_low[...], high))
    upper, lower = both_parts[:height], both_parts[height:]
    return jnp.concatenate(
        [upper[:, :depth] - lower[:, depth:], lower[:, :depth] + upper[:, depth:]], axis=1
    )


def coil_sum(real, imag, maps, kspace, mask, tables):
    total_real, total_imag = None, None
    for coil in range(maps.shape[0]):
        map_real, map_imag = maps[coil, 0, 0], maps[coil, 1, 0]
        image = jnp.concatenate(
            [map_real * real - map_imag * imag, map_real * imag + map_imag * real], axis=1
        )
        freq = spectrum(image, tables[:4])
        if kspace is not None:
            freq = freq - jnp.concatenate([kspace[coil, 0, 0], kspace[coil, 1, 0]], axis=1)
        back = spectrum(mask * freq, tables[4:])
        depth = real.shape[1]
        back_real, back_imag = back[:, :depth], back[:, depth:]
        part_real = map_real * back_real + map_imag * back_imag
        part_imag = map_real * back_imag - map_imag * back_real
        total_real = part_real if total_real is None else total_real + part_real
        total_imag = part_imag if total_imag is None else total_imag + part_imag
    return total_real, total_imag


def column(gathered, channel):
    return jnp.concatenate(
        [gathered[block, channel].astype(f32) for block in range(gathered.shape[0])], axis=0
    )


def data_kernel(place, gathered, maps, kspace, mask, *rest):
    tables, (parts_out, fields_out, padded) = rest[:8], rest[8:]
    height, depth = mask.shape
    pieces, window = parts_out.shape[0], parts_out.shape[2]
    own = window - 2 * reach
    weight = mask[...].astype(f32)
    weight = jnp.concatenate([weight, weight], axis=1)
    real, imag = column(gathered, 0), column(gathered, 1)
    padded[:, 0:8] = jnp.zeros((padded.shape[0], 8, depth), f32)
    padded[:, height + reach : height + reach + 8] = jnp.zeros((padded.shape[0], 8, depth), f32)
    for channel in range(fields_out.shape[1]):
        padded[channel, reach : reach + height] = column(gathered, channel)
    slabs = fields_out.shape[0]
    first = place[0] * (slabs * own)
    for piece in range(slabs):
        start = first + piece * own
        fields_out[piece] = padded[:, pl.ds(start, window), :].astype(bf16)
    total_real, total_imag = coil_sum(real, imag, maps, kspace, weight, tables)
    padded[0, reach : reach + height] = total_real
    padded[1, reach : reach + height] = total_imag
    for piece in range(pieces):
        parts_out[piece] = padded[0:2, piece * own : piece * own + window, :].astype(bf16)


def normal_kernel(gathered, pulled, maps, mask, *rest):
    tables, out = rest[:8], rest[8]
    weight = mask[...].astype(f32)
    weight = jnp.concatenate([weight, weight], axis=1)
    blocks, rows = out.shape[0], out.shape[2]
    for field in range(2):
        real = column(gathered, 2 + 2 * field) + column(pulled, 2 * field)
        imag = column(gathered, 3 + 2 * field) + column(pulled, 2 * field + 1)
        sums = coil_sum(real, imag, maps, None, weight, tables)
        for part in range(2):
            for block in range(blocks):
                out[block, 2 * field + part] = sums[part][block * rows : (block + 1) * rows].astype(bf16)


def banded(kernel, slices, form):
    outs, ins = kernel.shape[:2]
    order = {"in": (2, 0, 3, 4, 1), "mid": (3, 2, 0, 4, 1), "out": (3, 4, 2, 0, 1)}[form]
    taps, units = {"in": (1, 9), "mid": (3, 3), "out": (9, 1)}[form]
    small = jnp.transpose(kernel, order).reshape(taps * 3 * outs, units * ins)
    spread = np.kron(np.eye(units), np.tile(np.eye(ins), (1, slices)))
    wide = dot(small, jnp.asarray(spread, bf16)).reshape(taps, 1, 3, outs, -1)
    lane_slice = np.tile(np.repeat(np.arange(slices), ins), units)
    inside = (
        lane_slice[None, None, :]
        == (np.arange(slices)[:, None, None] + np.arange(3)[None, :, None] - 1)
    )
    chosen = wide * jnp.asarray(inside, f32)[None, :, :, None, :]
    return chosen.sum(2).astype(bf16).reshape(taps, slices * outs, -1)


def transposed(kernel):
    return jnp.swapaxes(jnp.flip(kernel, (2, 3, 4)), 0, 1)


def shifted(values, tap, depth):
    if tap == 1:
        return values
    lane = lax.broadcasted_iota(jnp.int32, (values.shape[0], depth), 1)
    edge, turn = (0, 1) if tap == 0 else (depth - 1, depth - 1)
    pieces = []
    for start in range(0, values.shape[1], depth):
        turned = pltpu.roll(values[:, start : start + depth], turn, 1)
        pieces.append(jnp.where(lane == edge, 0.0, turned))
    return jnp.concatenate(pieces, axis=1)


def conv_in(values, weights, depth):
    width = values.shape[1] - 2 * depth
    turned = [shifted(values, tap, depth) for tap in range(3)]
    stacked = jnp.concatenate(
        [turned[dz][:, dy * depth : dy * depth + width] for dy in range(3) for dz in range(3)],
        axis=0,
    )
    return dot(weights[0], stacked.astype(bf16))


def conv_mid(values, weights, depth):
    width = values.shape[1] - 2 * depth
    stacked = jnp.concatenate(
        [shifted(values, tap, depth).astype(bf16) for tap in range(3)], axis=0
    )
    total = None
    for dy in range(3):
        term = dot(weights[dy], stacked[:, dy * depth : dy * depth + width])
        total = term if total is None else total + term
    return total


def conv_out(values, weights, depth):
    width = values.shape[1] - 2 * depth
    taps, rows, inner = weights.shape
    products = dot(weights[...].reshape(taps * rows, inner), values.astype(bf16))
    total = None
    for dz in range(3):
        summed = None
        for dy in range(3):
            at = (dy * 3 + dz) * rows
            term = products[at : at + rows, dy * depth : dy * depth + width]
            summed = term if summed is None else summed + term
        term = shifted(summed, dz, depth)
        total = term if total is None else total + term
    return total


def conv_kernel(place, parts, fields, first, second, last, first_t, second_t, last_t,
                pulled_out, delta_out, work, rows_work):
    slices, channels, window, depth = fields.shape
    coils = parts.shape[0] // slices
    own = window - 2 * reach
    height = coils * slices * own
    row_base = place[0] * own - reach

    def load(values):
        work[...] = values.reshape(work.shape)
        return jnp.concatenate([work[:, row, :] for row in range(window)], axis=1)

    def cut(values, before, after):
        return values[:, before * depth : values.shape[1] - after * depth]

    def inside(values, offset):
        pieces = []
        for row in range(values.shape[1] // depth):
            at = row_base + offset + row
            keep = jnp.where((at >= 0) & (at < height), 1.0, 0.0).astype(f32)
            pieces.append(values[:, row * depth : (row + 1) * depth] * keep)
        return jnp.concatenate(pieces, axis=1)

    def store(values):
        for row in range(own):
            rows_work[:, row, :] = values[:, row * depth : (row + 1) * depth]
        return rows_work[...].reshape(slices, 2, own, depth)

    summed = parts[0:slices].astype(f32)
    for coil in range(1, coils):
        summed = summed + parts[coil * slices : (coil + 1) * slices].astype(f32)
    moved = load(-step_size * summed)
    relaxed = load(fields[:, 0:2].astype(f32)) + moved
    pre1 = conv_in(relaxed.astype(bf16).astype(f32), first, depth)
    sig1 = jax.nn.sigmoid(pre1)
    act1 = inside((pre1 * sig1), 1)
    slope1 = sig1 * (1.0 + pre1 * (1.0 - sig1))
    pre2 = conv_mid(act1, second, depth)
    sig2 = jax.nn.sigmoid(pre2)
    slope2 = inside(sig2 * (1.0 + pre2 * (1.0 - sig2)), 2)
    act2 = inside(cut(pre2 * sig2, 1, 1), 3)
    delta = conv_out(act2, last, depth) + cut(moved, reach, reach)
    delta_out[...] = store(delta)
    slope1 = inside(cut(slope1, 2, 2), 3)
    for field in range(2):
        probe = cut(load(fields[:, 2 + 2 * field : 4 + 2 * field].astype(f32)), 1, 1)
        grad2 = conv_in(probe, last_t, depth) * slope2
        grad1 = conv_mid(grad2, second_t, depth) * slope1
        grad0 = conv_out(grad1, first_t, depth)
        pulled_out[:, 2 * field : 2 * field + 2] = store(grad0).astype(bf16)


def on_device(coil_maps, kspace, sample_mask, iterate, probe_bits, loss_gradient, adjoint,
              kernel_first, kernel_second, kernel_last):
    height, depth = sample_mask.shape
    coils, slabs = lax.axis_size("coil"), lax.axis_size("slab")
    pieces = coils * slabs
    own = height // pieces
    window = own + 2 * reach
    rows = iterate.shape[2]
    my_coil, my_slab = lax.axis_index("coil"), lax.axis_index("slab")
    rank = my_coil * slabs + my_slab
    smem = pl.BlockSpec(memory_space=pltpu.SMEM)
    tables = fourier_tables(height, depth, -1.0) + fourier_tables(height, depth, 1.0)

    sign_field = (2 * probe_bits - 1).astype(f32)
    own_fields = jnp.concatenate([iterate, sign_field, adjoint], axis=0)[:, 0].astype(bf16)
    (gathered,) = exchange([(own_fields, ("coil",), "all")], 0)
    parts, fields = pl.pallas_call(
        data_kernel,
        out_shape=[
            jax.ShapeDtypeStruct((pieces, 2, window, depth), bf16),
            jax.ShapeDtypeStruct((slabs, 6, window, depth), bf16),
        ],
        in_specs=[smem] + [vmem] * 12,
        out_specs=[vmem] * 2,
        scratch_shapes=[pltpu.VMEM((6, height + 2 * reach + 8, depth), f32)],
    )(my_coil.reshape(1), gathered, coil_maps, kspace, sample_mask, *tables)
    parts, fields = exchange([(parts, both, "row"), (fields, ("slab",), "row")], 1)

    forward = [
        banded(kernel, slabs, form)
        for kernel, form in ((kernel_first, "in"), (kernel_second, "mid"), (kernel_last, "out"))
    ]
    backward = [
        banded(transposed(kernel), slabs, form)
        for kernel, form in ((kernel_first, "out"), (kernel_second, "mid"), (kernel_last, "in"))
    ]
    pulled, delta = pl.pallas_call(
        conv_kernel,
        out_shape=[
            jax.ShapeDtypeStruct((slabs, 4, own, depth), bf16),
            jax.ShapeDtypeStruct((slabs, 2, own, depth), f32),
        ],
        in_specs=[smem] + [vmem] * 8,
        out_specs=[vmem] * 2,
        scratch_shapes=[
            pltpu.VMEM((2 * slabs, window, depth), f32),
            pltpu.VMEM((2 * slabs, own, depth), f32),
        ],
    )(rank.reshape(1), parts, fields, *forward, *backward)
    pulled, delta = exchange([(pulled, both, "slab"), (delta, ("slab",), "row")], 2)
    new_iterate = iterate + jnp.swapaxes(delta, 0, 1).reshape(2, 1, rows, depth)

    sums = pl.pallas_call(
        normal_kernel,
        out_shape=jax.ShapeDtypeStruct((coils, 4, rows, depth), bf16),
        in_specs=[vmem] * 12,
        out_specs=vmem,
    )(gathered, pulled, coil_maps, sample_mask, *tables)
    (sums,) = exchange([(sums, ("coil",), "row")], 3)
    mine = lax.dynamic_slice_in_dim(pulled, my_coil * slabs, slabs, 0).astype(f32)
    mine = jnp.swapaxes(mine, 0, 1).reshape(4, rows, depth)
    step = mine - step_size * sums.astype(f32).sum(0)
    probe_pullback = sign_field + step[0:2, None]
    adjoint_next = loss_gradient + (adjoint + step[2:4, None])
    return new_iterate, probe_pullback, adjoint_next


def solution(mesh):
    split_coils = P("coil", None, "slab", None, None)
    image = P(None, "slab", "coil", None)
    return jax.shard_map(
        on_device,
        mesh=mesh,
        in_specs=(split_coils, split_coils, P(), image, image, image, image, P(), P(), P()),
        out_specs=(image, image, image),
        check_vma=False,
    )
```

time: 798 us -> 85.3 us (0.11); the launches traced: 785 us -> 84.8 us
  matrix products: 413 us -> 1.15 us
  local copies, waits for them, and re-layouts: 181 us -> 2.55 us
  starting transfers between devices: 73.4 us -> 0 us
  Pallas kernels: 0 us -> 71.8 us
  other arithmetic: 45.8 us -> 8.39 us
  waiting for transfers between devices: 35 us -> 0 us
  blocking collectives: 20.4 us -> 0 us
  between operations: 16 us -> 0.93 us
    conv_general_dilated x6 -> x0, matrix products: 347 us -> none  [convolve_local(): lax.conv_general_dilated(haloed, kernel, (1, 1, 1), ((0, 0), (0, 0), (1,...]
    conv_general_dilated x21 -> x0, local copies, waits for them, and re-layouts: 108 us -> none  [convolve_local(): lax.conv_general_dilated(haloed, kernel, (1, 1, 1), ((0, 0), (0, 0), (1,...]
    ppermute x24 -> x0, starting transfers between devices: 73.3 us -> none  [the longest x12 57.8 us: with_halo(): lax.ppermute(tail, axis, [(i, (i + 1) % count) for i in range(ends)])]
    pallas_call x0 -> x7, Pallas kernels: none -> 71.8 us  [the longest x4 51.2 us: exchange(): pl.pallas_call(kernel, out_shape=outs, in_specs=[vmem] * count, out_specs...]
    dot_general x64 -> x6, matrix products: 66.4 us -> 1.15 us  [dot(): return jnp.dot(left, right, preferred_element_type=f32)]
    psum x2 -> x0, waiting for transfers between devices: 30.6 us -> none  [the longest x1 30.6 us: on_device(): summed = lax.psum(partial_sum, 'coil')]
    ppermute x16 -> x0, local copies, waits for them, and re-layouts: 29 us -> none  [the longest x8 15.7 us: with_halo(): lax.ppermute(tail, axis, [(i, (i + 1) % count) for i in range(ends)])]
    concatenate x12 -> x0, other arithmetic: 27.7 us -> none  [with_halo(): jnp.concatenate([lax.ppermute(tail, axis, [(i, (i + 1) % count) for i in...]
  transfers between devices with their start and end apart: 26 -> 0, of which waited for: 6 -> 0; matrix products, arithmetic and copies ran while one was open for 29% -> 0% of each run, Pallas kernels for 0% -> 0%
where the time goes in v1:
time: 85.3 us; the launch traced here: 84.8 us
  Pallas kernels  71.8 us (84%)
  other arithmetic  8.39 us (10%)
  local copies, waits for them, and re-layouts  2.55 us (3%)
  matrix products  1.15 us (1%)
  between operations  0.93 us (1%)
    pallas_call x4, Pallas kernels, exchange(): pl.pallas_call(kernel, out_shape=outs, in_specs=[vmem] * count, out_specs...  51.2 us
    pallas_call x1, Pallas kernels, on_device(): pl.pallas_call(conv_kernel, out_shape=[jax.ShapeDtypeStruct((slabs, 4, ow...  8.32 us
    pallas_call x1, Pallas kernels, on_device(): pl.pallas_call(normal_kernel, out_shape=jax.ShapeDtypeStruct((coils, 4, r...  6.83 us
    pallas_call x1, Pallas kernels, on_device(): pl.pallas_call(data_kernel, out_shape=[jax.ShapeDtypeStruct((pieces, 2, w...  5.46 us
    reduce_sum x3, other arithmetic, banded(): return chosen.sum(2).astype(bf16).reshape(taps, slices * outs, -1)  2.83 us
    another operation x2, other arithmetic  1.74 us

profile of v1, /device:TPU:0, one launch (start us, length us, event | category | flops | bytes accessed | tf_op | source)
XLA Modules:
  0.0 84.8 jit_solution(9186098526540178617)
XLA Ops:
  0.6 0.9 %bitcast_convert_fusion = (bf16[2,1,64,128]{3,2,0,1:T(8,128)(2,1)S(1)}, bf16[2,1,64,128]{3,2,0,1:T(8,128)(2,1)S(1)}) fusion(f32[2,1,64,128]{3,2,1,0:T(8,128)} %param.36, f32[2,1,64,128]{3,2,1,0:T(8,128)} %param.33), kind=kLoop, calls=%fused_computation.26 | loop fusion | flops 32768 | bytes 196608 | tf_op jit(solution)/shard_map/convert.4
  1.5 0.9 %fusion.9 = bf16[2,1,64,128]{3,2,0,1:T(8,128)(2,1)S(1)} fusion(s32[2,1,64,128]{3,2,1,0:T(8,128)} %param.34), kind=kLoop, calls=%fused_computation.31 | loop fusion | flops 65536 | bytes 98304 | tf_op jit(solution)/shard_map/convert.3
  2.4 0.6 maximum_bitcast_fusion.refs_0_
  3.0 10.8 %shard_map.301.gathered = bf16[4,6,64,128]{3,2,1,0:T(8,128)(2,1)} custom-call(bf16[6,64,128]{2,1,0:T(8,128)(2,1)} %maximum_bitcast_fusion.refs_0_), custom_call_target="tpu_custom_call" | custom-call | tf_op jit(solution)/shard_map/pallas_call | solution.py:99
  13.8 0.0 copy-start
  13.8 5.5 %shard_map.302 = (bf16[32,2,16,128]{3,2,1,0:T(8,128)(2,1)}, bf16[8,6,16,128]{3,2,1,0:T(8,128)(2,1)}) custom-call(s32[1]{0:T(128)} %bitcast.2.place, bf16[4,6,64,128]{3,2,1,0:T(8,128)(2,1)} %shard_map.301.gathered, f32[2,2,1,256,128]{4,3,2,1,0:T(8,128)} %maps.3, f32[2,2,1,256,128]{4,3,2,1,0:T(8,128)} %kspace.1, s32[256,128]{1,0:T(8,128)} %mask.3, ...), custom_call_target="tpu_custom_call" | custom-call | tf_op jit(solution)/shard_map/pallas_call | solution.py:352
  19.3 0.0 copy-start.1
  19.3 17.9 %shard_map.303 = (bf16[32,2,16,128]{3,2,1,0:T(8,128)(2,1)}, bf16[8,6,16,128]{3,2,1,0:T(8,128)(2,1)}) custom-call(bf16[32,2,16,128]{3,2,1,0:T(8,128)(2,1)} %get-tuple-element.11.refs_0_, bf16[8,6,16,128]{3,2,1,0:T(8,128)(2,1)} %get-tuple-element.12.refs_1_), custom_call_target="tpu_custom_call" | custom-call | tf_op jit(solution)/shard_map/pallas_call | solution.py:99
  37.2 0.0 copy-done
  37.3 0.1 copy.70
  37.3 0.1 reshape.151
  37.5 0.0 copy-done.1
  37.5 0.2 convolution_bitcast_fusion.1
  37.7 0.0 copy-start.6
  37.8 0.3 convolution_bitcast_fusion
  38.1 0.5 copy-done.6
  38.6 0.0 copy-start.9
  38.6 0.0 copy-start.11
  38.6 0.0 copy-start.5
  38.6 0.0 copy-start.13
  38.6 2.0 %multiply_reduce_fusion = (bf16[3,8,24,576]{3,2,1,0:T(8,128)(2,1)}, bf16[3,8,24,576]{3,2,1,0:T(8,128)(2,1)}) fusion(f32[3,3,24,576]{3,2,1,0:T(8,128)S(1)} %convolution_bitcast_fusion, f32[8,3,576]{2,1,0:T(4,128)S(1)} %copy-done.6, f32[3,3,24,576]{3,2,1,0:T(8,128)S(1)} %convolution_bitcast_fusion.1), kind=kLoop, calls=%fused_computation | loop fusion | flops 3317760 | bytes 2377728 | tf_op jit(solution)/shard_map/reduce_sum | solution.py:227
  40.6 0.0 copy-done.9
  40.6 0.0 copy-done.11
  40.7 0.0 copy-start.10
  40.7 0.1 convolution_bitcast_fusion.2
  40.8 0.0 copy-start.12
  40.9 0.0 copy-done.5
  40.9 0.1 convolution_bitcast_fusion.3
  41.0 0.0 copy-done.13
  41.1 0.1 multiply_reduce_fusion.4
  41.1 0.1 copy.73
  41.2 0.7 convert_element_type.123.last
  41.9 0.1 copy.76
  42.0 0.7 convert_element_type.125.first_t
  42.7 0.0 copy-done.10
  42.7 0.2 convolution_bitcast_fusion.4
  43.0 0.2 convolution_bitcast_fusion.5
  43.1 0.0 copy-done.12
  43.2 0.8 multiply_reduce_fusion.2
  43.9 8.3 %shard_map.304 = (bf16[8,4,8,128]{3,2,1,0:T(8,128)(2,1)}, f32[8,2,8,128]{3,2,1,0:T(8,128)}) custom-call(s32[1]{0:T(128)} %bitcast.1.place, bf16[32,2,16,128]{3,2,1,0:T(8,128)(2,1)} %get-tuple-element.13.parts, bf16[8,6,16,128]{3,2,1,0:T(8,128)(2,1)} %get-tuple-element.14.fields, bf16[1,192,144]{2,1,0:T(8,128)(2,1)} %bitcast.110, ...), custom_call_target="tpu_custom_call" | custom-call | tf_op jit(solution)/shard_map/pallas_call | solution.py:372
  52.2 14.2 %shard_map.305 = (bf16[32,4,8,128]{3,2,1,0:T(8,128)(2,1)}, f32[8,2,8,128]{3,2,1,0:T(8,128)}) custom-call(bf16[8,4,8,128]{3,2,1,0:T(8,128)(2,1)} %get-tuple-element.15.refs_0_, f32[8,2,8,128]{3,2,1,0:T(8,128)} %get-tuple-element.16.refs_1_), custom_call_target="tpu_custom_call" | custom-call | tf_op jit(solution)/shard_map/pallas_call | solution.py:99
  66.5 6.8 %shard_map.306.refs_0_ = bf16[4,4,64,128]{3,2,1,0:T(8,128)(2,1)} custom-call(bf16[4,6,64,128]{3,2,1,0:T(8,128)(2,1)} %shard_map.301.gathered, bf16[32,4,8,128]{3,2,1,0:T(8,128)(2,1)} %get-tuple-element.18.pulled, f32[2,2,1,256,128]{4,3,2,1,0:T(8,128)} %maps.3, s32[256,128]{1,0:T(8,128)} %mask.3, bf16[256,256]{1,0:T(8,128)(2,1)} %constant.59.rest_0_, ...), custom_call_target="tpu_custom_call" | custom-call | tf_op jit(solution)/shard_map/pallas_call | solution.py:388
  73.3 0.0 copy-start.2
  73.3 0.0 copy-start.4
  73.3 0.0 copy-start.7
  73.3 0.0 copy-start.3
  73.4 0.0 copy-start.8
  73.4 8.2 %shard_map.307 = bf16[4,4,64,128]{3,2,1,0:T(8,128)(2,1)} custom-call(bf16[4,4,64,128]{3,2,1,0:T(8,128)(2,1)} %shard_map.306.refs_0_), custom_call_target="tpu_custom_call" | custom-call | tf_op jit(solution)/shard_map/pallas_call | solution.py:99
  81.6 1.0 %convert_reduce_fusion = f32[4,64,128]{2,1,0:T(8,128)S(1)} fusion(bf16[4,4,64,128]{3,2,1,0:T(8,128)(2,1)} %shard_map.307), kind=kLoop, calls=%fused_computation.10 | loop fusion | flops 229376 | bytes 393216 | tf_op jit(solution)/shard_map/reduce_sum | solution.py:397
  82.6 0.9 %bitcast_subtract_fusion = f32[4,64,128]{2,1,0:T(8,128)S(1)} fusion(f32[4,64,128]{2,1,0:T(8,128)S(1)} %convert_reduce_fusion, bf16[32,4,8,128]{3,2,1,0:T(8,128)(2,1)} %get-tuple-element.18.pulled, s32[]{:T(128)S(6)} %select_n.3), kind=kLoop, calls=%fused_computation.14 | loop fusion | flops 98304 | bytes 327684 | tf_op jit(solution)/shard_map/sub | solution.py:397
  83.4 0.0 copy-done.2
  83.5 0.0 copy-done.4
  83.5 0.0 copy-done.7
  83.5 0.7 fusion.3
  84.2 0.0 copy-done.3
  84.2 0.0 copy-done.8
  84.2 0.6 fusion.6
  (7 shorter events, 0.2 us)
Async XLA Ops:
  13.8 23.4 %copy-start = (bf16[24,24,3,3,3]{1,0,4,3,2:T(8,128)(2,1)S(1)}, bf16[24,24,3,3,3]{1,0,4,3,2:T(8,128)(2,1)}, u32[]{:S(2)}) copy-start(bf16[24,24,3,3,3]{1,0,4,3,2:T(8,128)(2,1)} %param.38) | copy-start | bytes 93316
  19.3 18.2 %copy-start.1 = (bf16[72,576,1,1]{1,0,3,2:T(8,128)(2,1)S(1)}, bf16[72,576,1,1]{1,0,3,2:T(8,128)(2,1)}, u32[]{:S(2)}) copy-start(bf16[72,576,1,1]{1,0,3,2:T(8,128)(2,1)} %constant.76) | copy-start | bytes 248836
  37.7 0.9 %copy-start.6 = (f32[8,3,576]{2,1,0:T(4,128)S(1)}, f32[8,3,576]{2,1,0:T(4,128)}, u32[]{:S(2)}) copy-start(f32[8,3,576]{2,1,0:T(4,128)} %constant.50.clone) | copy-start | bytes 165892
  38.6 2.0 %copy-start.9 = (bf16[24,2,3,3,3]{0,1,4,3,2:T(2,128)(2,1)S(1)}, bf16[24,2,3,3,3]{0,1,4,3,2:T(2,128)(2,1)}, u32[]{:S(2)}) copy-start(bf16[24,2,3,3,3]{0,1,4,3,2:T(2,128)(2,1)} %param.37) | copy-start | bytes 7780
  38.6 2.0 %copy-start.11 = (bf16[24,192,1,1]{1,0,3,2:T(8,128)(2,1)S(1)}, bf16[24,192,1,1]{1,0,3,2:T(8,128)(2,1)}, u32[]{:S(2)}) copy-start(bf16[24,192,1,1]{1,0,3,2:T(8,128)(2,1)} %constant.77) | copy-start | bytes 27652
  38.6 2.2 %copy-start.5 = (bf16[2,24,3,3,3]{1,0,4,3,2:T(2,128)(2,1)S(1)}, bf16[2,24,3,3,3]{1,0,4,3,2:T(2,128)(2,1)}, u32[]{:S(2)}) copy-start(bf16[2,24,3,3,3]{1,0,4,3,2:T(2,128)(2,1)} %param.39) | copy-start | bytes 7780
  38.6 2.4 %copy-start.13 = (f32[8,3,192]{2,0,1:T(8,128)S(1)}, f32[8,3,192]{2,0,1:T(8,128)}, u32[]{:S(2)}) copy-start(f32[8,3,192]{2,0,1:T(8,128)} %constant.52.clone) | copy-start | bytes 55300
  40.7 2.1 %copy-start.10 = (bf16[18,144,1]{1,0,2:T(8,128)(2,1)S(1)}, bf16[18,144,1]{1,0,2:T(8,128)(2,1)}, u32[]{:S(2)}) copy-start(bf16[18,144,1]{1,0,2:T(8,128)(2,1)} %constant.75) | copy-start | bytes 15556
  40.8 2.3 %copy-start.12 = (f32[8,3,144]{2,1,0:T(4,128)S(1)}, f32[8,3,144]{2,1,0:T(4,128)}, u32[]{:S(2)}) copy-start(f32[8,3,144]{2,1,0:T(4,128)} %constant.48.clone) | copy-start | bytes 41476
  73.3 10.1 %copy-start.2 = (f32[2,1,64,128]{3,2,1,0:T(8,128)S(1)}, f32[2,1,64,128]{3,2,1,0:T(8,128)}, u32[]{:S(2)}) copy-start(f32[2,1,64,128]{3,2,1,0:T(8,128)} %param.36) | copy-start | bytes 196612
  73.3 10.1 %copy-start.4 = (s32[2,1,64,128]{3,2,1,0:T(8,128)S(1)}, s32[2,1,64,128]{3,2,1,0:T(8,128)}, u32[]{:S(2)}) copy-start(s32[2,1,64,128]{3,2,1,0:T(8,128)} %param.34) | copy-start | bytes 196612
  73.3 10.1 %copy-start.7 = (f32[2,1,64,128]{3,2,1,0:T(8,128)S(1)}, f32[2,1,64,128]{3,2,1,0:T(8,128)}, u32[]{:S(2)}) copy-start(f32[2,1,64,128]{3,2,1,0:T(8,128)} %param.35) | copy-start | bytes 196612
  73.3 10.8 %copy-start.3 = (f32[2,1,64,128]{3,2,1,0:T(8,128)S(1)}, f32[2,1,64,128]{3,2,1,0:T(8,128)}, u32[]{:S(2)}) copy-start(f32[2,1,64,128]{3,2,1,0:T(8,128)} %param.33) | copy-start | bytes 196612
  73.4 10.8 %copy-start.8 = (f32[8,2,8,128]{3,2,1,0:T(8,128)S(1)}, f32[8,2,8,128]{3,2,1,0:T(8,128)}, u32[]{:S(2)}) copy-start(f32[8,2,8,128]{3,2,1,0:T(8,128)} %get-tuple-element.17) | copy-start | bytes 196612

commit v2 on v1

v2 whole, which is shorter than its diff:
```python
import math

import jax
import jax.numpy as jnp
import numpy as np
from jax import lax
from jax.experimental import pallas as pl
from jax.experimental.pallas import tpu as pltpu
from jax.sharding import PartitionSpec as P

step_size = 0.8
reach = 4
both = ("coil", "slab")
f32 = jnp.float32
bf16 = jnp.bfloat16
vmem = pl.BlockSpec(memory_space=pltpu.VMEM)
MESH = pl.DeviceIdType.MESH


class Channel:
    def __init__(self, axes, how, source, target, send_sem, recv_sem):
        self.axes, self.how, self.source, self.target = axes, how, source, target
        self.send_sem, self.recv_sem = send_sem, recv_sem
        self.size = math.prod(lax.axis_size(axis) for axis in axes)
        self.mine = rank_of(axes)

    def row(self, rank):
        if self.how == "all":
            return self.source
        if self.how == "slab":
            return self.source.at[place_of(self.axes, rank)[1]]
        return self.source.at[rank]

    def copy(self, source_rank, target_row, device_rank, step):
        return pltpu.make_async_remote_copy(
            src_ref=self.row(source_rank),
            dst_ref=self.target.at[target_row],
            send_sem=self.send_sem.at[step],
            recv_sem=self.recv_sem.at[step],
            device_id=place_of(self.axes, device_rank),
            device_id_type=MESH,
        )

    def start(self):
        def send(step, carry):
            rank = lax.rem(self.mine + step, self.size)
            self.copy(rank, self.mine, rank, step).start()
            return carry

        lax.fori_loop(1, self.size, send, 0)
        self.target[self.mine] = self.row(self.mine)[...]

    def finish(self):
        def wait(step, carry):
            rank = lax.rem(self.mine + self.size - step, self.size)
            self.copy(self.mine, rank, rank, step).wait()
            return carry

        lax.fori_loop(1, self.size, wait, 0)


def rank_of(axes):
    if axes == both:
        return lax.axis_index("coil") * lax.axis_size("slab") + lax.axis_index("slab")
    return lax.axis_index(axes[0])


def place_of(axes, rank):
    slabs = lax.axis_size("slab")
    if axes == both:
        return lax.div(rank, slabs), lax.rem(rank, slabs)
    return (rank, lax.axis_index("slab")) if axes == ("coil",) else (lax.axis_index("coil"), rank)


def greet_all():
    barrier = pltpu.get_barrier_semaphore()
    size = lax.axis_size("coil") * lax.axis_size("slab")

    def greet(step, carry):
        rank = lax.rem(rank_of(both) + step, size)
        pl.semaphore_signal(barrier, inc=1, device_id=place_of(both, rank), device_id_type=MESH)
        return carry

    lax.fori_loop(1, size, greet, 0)
    return barrier, size - 1


def split(table):
    high = jnp.asarray(table, f32).astype(bf16)
    return high, (jnp.asarray(table, f32) - high.astype(f32)).astype(bf16)


def fourier_tables(height, depth, sign):
    def parts(length):
        counter = np.arange(length)
        angles = (counter[:, None] * counter[None, :] % length) * (2.0 * np.pi / length)
        return np.cos(angles) / np.sqrt(length), sign * np.sin(angles) / np.sqrt(length)

    depth_cos, depth_sin = parts(depth)
    height_cos, height_sin = parts(height)
    along = np.block([[depth_cos, depth_sin], [-depth_sin, depth_cos]])
    down = np.concatenate([height_cos, height_sin], axis=0)
    return split(along) + split(down)


def dot(left, right):
    return jnp.dot(left, right, preferred_element_type=f32)


def halves(values):
    high = values.astype(bf16)
    return high, (values - high.astype(f32)).astype(bf16)


def spectrum(values, tables):
    along_high, along_low, down_high, down_low = tables
    height, depth = values.shape[0], values.shape[1] // 2
    high, low = halves(values)
    high, low = halves(
        dot(high, along_high[...]) + (dot(low, along_high[...]) + dot(high, along_low[...]))
    )
    both_parts = dot(down_high[...], high) + (dot(down_high[...], low) + dot(down_low[...], high))
    upper, lower = both_parts[:height], both_parts[height:]
    return jnp.concatenate(
        [upper[:, :depth] - lower[:, depth:], lower[:, :depth] + upper[:, depth:]], axis=1
    )


def coil_term(real, imag, coil, maps, kspace, mask, tables):
    depth = real.shape[1]
    map_real, map_imag = maps[coil, 0, 0], maps[coil, 1, 0]
    image = jnp.concatenate(
        [map_real * real - map_imag * imag, map_real * imag + map_imag * real], axis=1
    )
    freq = spectrum(image, tables[:4])
    if kspace is not None:
        freq = freq - jnp.concatenate([kspace[coil, 0, 0], kspace[coil, 1, 0]], axis=1)
    back = spectrum(mask * freq, tables[4:])
    back_real, back_imag = back[:, :depth], back[:, depth:]
    return (
        map_real * back_real + map_imag * back_imag,
        map_real * back_imag - map_imag * back_real,
    )


def column(gathered, channel):
    return jnp.concatenate(
        [gathered[block, channel].astype(f32) for block in range(gathered.shape[0])], axis=0
    )


def banded(kernel, slices, form):
    outs, ins = kernel.shape[:2]
    order = {"in": (2, 0, 3, 4, 1), "mid": (3, 2, 0, 4, 1), "out": (3, 4, 2, 0, 1)}[form]
    taps, units = {"in": (1, 9), "mid": (3, 3), "out": (9, 1)}[form]
    small = jnp.transpose(kernel, order).reshape(taps * 3 * outs, units * ins)
    spread = np.kron(np.eye(units), np.tile(np.eye(ins), (1, slices)))
    wide = dot(small, jnp.asarray(spread, bf16)).reshape(taps, 1, 3, outs, -1)
    lane_slice = np.tile(np.repeat(np.arange(slices), ins), units)
    inside = (
        lane_slice[None, None, :]
        == (np.arange(slices)[:, None, None] + np.arange(3)[None, :, None] - 1)
    )
    chosen = wide * jnp.asarray(inside, f32)[None, :, :, None, :]
    return chosen.sum(2).astype(bf16).reshape(taps, slices * outs, -1)


def transposed(kernel):
    return jnp.swapaxes(jnp.flip(kernel, (2, 3, 4)), 0, 1)


def shifted(values, tap, depth):
    if tap == 1:
        return values
    lane = lax.broadcasted_iota(jnp.int32, (values.shape[0], depth), 1)
    edge, turn = (0, 1) if tap == 0 else (depth - 1, depth - 1)
    pieces = []
    for start in range(0, values.shape[1], depth):
        turned = pltpu.roll(values[:, start : start + depth], turn, 1)
        pieces.append(jnp.where(lane == edge, 0.0, turned))
    return jnp.concatenate(pieces, axis=1)


def conv_in(values, weights, depth):
    width = values.shape[1] - 2 * depth
    turned = [shifted(values, tap, depth) for tap in range(3)]
    stacked = jnp.concatenate(
        [turned[dz][:, dy * depth : dy * depth + width] for dy in range(3) for dz in range(3)],
        axis=0,
    )
    return dot(weights[0], stacked.astype(bf16))


def conv_mid(values, weights, depth):
    width = values.shape[1] - 2 * depth
    stacked = jnp.concatenate(
        [shifted(values, tap, depth).astype(bf16) for tap in range(3)], axis=0
    )
    total = None
    for dy in range(3):
        term = dot(weights[dy], stacked[:, dy * depth : dy * depth + width])
        total = term if total is None else total + term
    return total


def conv_out(values, weights, depth):
    width = values.shape[1] - 2 * depth
    taps, rows, inner = weights.shape
    products = dot(weights[...].reshape(taps * rows, inner), values.astype(bf16))
    total = None
    for dz in range(3):
        summed = None
        for dy in range(3):
            at = (dy * 3 + dz) * rows
            term = products[at : at + rows, dy * depth : dy * depth + width]
            summed = term if summed is None else summed + term
        term = shifted(summed, dz, depth)
        total = term if total is None else total + term
    return total


def step_kernel(maps, kspace, mask, iterate, probe_bits, loss_gradient, adjoint, *rest):
    tables, weights, rest = rest[:8], rest[8:14], rest[14:]
    first, second, last, first_t, second_t, last_t = weights
    new_out, probe_out, adjoint_out = rest[:3]
    (padded, work, rows_work, own_iterate, own_fields, all_iterate, all_fields, parts_send, parts,
     fields_send, fields, delta_send, delta, pulled_send, pulled, sums_send, sums) = rest[3:20]
    sems = rest[20:]
    channels = []
    for index, (axes, how, source, target) in enumerate((
        (("coil",), "all", own_iterate, all_iterate),
        (("coil",), "all", own_fields, all_fields),
        (("slab",), "row", fields_send, fields),
        (both, "row", parts_send, parts),
        (("slab",), "row", delta_send, delta),
        (both, "slab", pulled_send.at[0], pulled.at[0]),
        (both, "slab", pulled_send.at[1], pulled.at[1]),
        (("coil",), "row", sums_send.at[0], sums.at[0]),
        (("coil",), "row", sums_send.at[1], sums.at[1]),
    )):
        channels.append(Channel(axes, how, source, target, sems[2 * index], sems[2 * index + 1]))
    (iterate_way, field_way, window_way, part_way, delta_way, *later) = channels
    pulled_ways, sum_ways = later[:2], later[2:]

    height, depth = mask.shape
    coils, rows = all_iterate.shape[0], all_iterate.shape[2]
    pieces, _, window, _ = parts.shape
    slices = fields.shape[0]
    own = window - 2 * reach
    my_coil = lax.axis_index("coil")
    row_base = rank_of(both) * own - reach

    barrier, arrivals = greet_all()
    sign = (2 * probe_bits[...] - 1).astype(f32)
    own_iterate[...] = iterate[:, 0].astype(bf16)
    own_fields[0:2] = sign[:, 0].astype(bf16)
    own_fields[2:4] = adjoint[:, 0].astype(bf16)
    edge = jnp.zeros((6, 8, depth), f32)
    padded[:, 0:8] = edge
    padded[:, height + reach : height + reach + 8] = edge
    weight = mask[...].astype(f32)
    weight = jnp.concatenate([weight, weight], axis=1)
    pl.semaphore_wait(barrier, arrivals)
    iterate_way.start()
    field_way.start()
    iterate_way.finish()

    real, imag = column(all_iterate, 0), column(all_iterate, 1)
    total_real, total_imag = coil_term(real, imag, 0, maps, kspace, weight, tables)
    field_way.finish()
    padded[0, reach : reach + height] = real
    padded[1, reach : reach + height] = imag
    for channel in range(4):
        padded[2 + channel, reach : reach + height] = column(all_fields, channel)
    for piece in range(slices):
        start = my_coil * (slices * own) + piece * own
        fields_send[piece] = padded[:, pl.ds(start, window), :].astype(bf16)
    window_way.start()
    for coil in range(1, maps.shape[0]):
        more_real, more_imag = coil_term(real, imag, coil, maps, kspace, weight, tables)
        total_real, total_imag = total_real + more_real, total_imag + more_imag
    padded[0, reach : reach + height] = total_real
    padded[1, reach : reach + height] = total_imag
    for piece in range(pieces):
        parts_send[piece] = padded[0:2, piece * own : piece * own + window, :].astype(bf16)
    part_way.start()

    def load(values):
        work[...] = values.reshape(work.shape)
        return jnp.concatenate([work[:, row, :] for row in range(window)], axis=1)

    def cut(values, before, after):
        return values[:, before * depth : values.shape[1] - after * depth]

    def inside(values, offset):
        blocks = []
        for row in range(values.shape[1] // depth):
            at = row_base + offset + row
            keep = jnp.where((at >= 0) & (at < height), 1.0, 0.0).astype(f32)
            blocks.append(values[:, row * depth : (row + 1) * depth] * keep)
        return jnp.concatenate(blocks, axis=1)

    def store(values):
        for row in range(own):
            rows_work[:, row, :] = values[:, row * depth : (row + 1) * depth]
        return rows_work[...].reshape(slices, 2, own, depth)

    window_way.finish()
    started = load(fields[:, 0:2].astype(f32))
    grads = []
    for field in range(2):
        probe = cut(load(fields[:, 2 + 2 * field : 4 + 2 * field].astype(f32)), 1, 1)
        grads.append(conv_in(probe, last_t, depth))
    part_way.finish()
    summed = parts[0:slices].astype(f32)
    for coil in range(1, coils):
        summed = summed + parts[coil * slices : (coil + 1) * slices].astype(f32)
    moved = load(-step_size * summed)
    relaxed = started + moved
    pre1 = conv_in(relaxed.astype(bf16).astype(f32), first, depth)
    sig1 = jax.nn.sigmoid(pre1)
    act1 = inside(pre1 * sig1, 1)
    slope1 = inside(cut(sig1 * (1.0 + pre1 * (1.0 - sig1)), 2, 2), 3)
    pre2 = conv_mid(act1, second, depth)
    sig2 = jax.nn.sigmoid(pre2)
    slope2 = inside(sig2 * (1.0 + pre2 * (1.0 - sig2)), 2)
    for field in range(2):
        grad1 = conv_mid(grads[field] * slope2, second_t, depth) * slope1
        pulled_send[field] = store(conv_out(grad1, first_t, depth)).astype(bf16)
        pulled_ways[field].start()
    act2 = inside(cut(pre2 * sig2, 1, 1), 3)
    delta_send[...] = store(conv_out(act2, last, depth) + cut(moved, reach, reach))
    delta_way.start()

    for field in range(2):
        pulled_ways[field].finish()
        real = column(all_fields, 2 * field) + column(pulled.at[field], 0)
        imag = column(all_fields, 2 * field + 1) + column(pulled.at[field], 1)
        total = None
        for coil in range(maps.shape[0]):
            term = coil_term(real, imag, coil, maps, None, weight, tables)
            total = term if total is None else (total[0] + term[0], total[1] + term[1])
        for part in range(2):
            for block in range(coils):
                at = block * rows
                sums_send[field, block, part] = total[part][at : at + rows].astype(bf16)
        sum_ways[field].start()

    delta_way.finish()
    for part in range(2):
        for piece in range(slices):
            at = piece * own
            new_out[part, 0, at : at + own] = iterate[part, 0, at : at + own] + delta[piece, part]
    starts = (sign, loss_gradient[...] + adjoint[...])
    for field, out in ((0, probe_out), (1, adjoint_out)):
        sum_ways[field].finish()
        for part in range(2):
            added = sums[field, 0, part].astype(f32)
            for block in range(1, coils):
                added = added + sums[field, block, part].astype(f32)
            mine = jnp.concatenate(
                [
                    pulled[field, my_coil * slices + piece, part].astype(f32)
                    for piece in range(slices)
                ],
                axis=0,
            )
            out[part, 0] = starts[field][part, 0] + (mine - step_size * added)


def on_device(coil_maps, kspace, sample_mask, iterate, probe_bits, loss_gradient, adjoint,
              kernel_first, kernel_second, kernel_last):
    height, depth = sample_mask.shape
    coils, slabs = lax.axis_size("coil"), lax.axis_size("slab")
    pieces = coils * slabs
    own = height // pieces
    window = own + 2 * reach
    rows = iterate.shape[2]
    tables = fourier_tables(height, depth, -1.0) + fourier_tables(height, depth, 1.0)
    forward = [
        banded(kernel, slabs, form)
        for kernel, form in ((kernel_first, "in"), (kernel_second, "mid"), (kernel_last, "out"))
    ]
    backward = [
        banded(transposed(kernel), slabs, form)
        for kernel, form in ((kernel_first, "out"), (kernel_second, "mid"), (kernel_last, "in"))
    ]
    buffers = [
        ((6, height + 2 * reach + 8, depth), f32),
        ((2 * slabs, window, depth), f32),
        ((2 * slabs, own, depth), f32),
        ((2, rows, depth), bf16),
        ((4, rows, depth), bf16),
        ((coils, 2, rows, depth), bf16),
        ((coils, 4, rows, depth), bf16),
        ((pieces, 2, window, depth), bf16),
        ((pieces, 2, window, depth), bf16),
        ((slabs, 6, window, depth), bf16),
        ((slabs, 6, window, depth), bf16),
        ((slabs, 2, own, depth), f32),
        ((slabs, 2, own, depth), f32),
        ((2, slabs, 2, own, depth), bf16),
        ((2, pieces, 2, own, depth), bf16),
        ((2, coils, 2, rows, depth), bf16),
        ((2, coils, 2, rows, depth), bf16),
    ]
    ways = (coils, coils, slabs, pieces, slabs, pieces, pieces, coils, coils)
    return pl.pallas_call(
        step_kernel,
        out_shape=[jax.ShapeDtypeStruct(iterate.shape, f32)] * 3,
        in_specs=[vmem] * 21,
        out_specs=[vmem] * 3,
        scratch_shapes=[pltpu.VMEM(shape, kind) for shape, kind in buffers]
        + [pltpu.SemaphoreType.DMA((size,)) for size in ways for _ in range(2)],
        compiler_params=pltpu.CompilerParams(collective_id=0, has_side_effects=True),
    )(coil_maps, kspace, sample_mask, iterate, probe_bits, loss_gradient, adjoint,
      *tables, *forward, *backward)


def solution(mesh):
    split_coils = P("coil", None, "slab", None, None)
    image = P(None, "slab", "coil", None)
    return jax.shard_map(
        on_device,
        mesh=mesh,
        in_specs=(split_coils, split_coils, P(), image, image, image, image, P(), P(), P()),
        out_specs=(image, image, image),
        check_vma=False,
    )
```

time: 85.3 us -> 61.3 us (0.72)
  Pallas kernels: 71.8 us -> 48.3 us
  other arithmetic: 8.39 us -> 2.83 us
  local copies, waits for them, and re-layouts: 2.55 us -> 7.92 us
    pallas_call x7 -> x1, Pallas kernels: 71.8 us -> 48.3 us  [on_device(): pl.pallas_call(step_kernel, out_shape=[jax.ShapeDtypeStruct(iterate.shape...]
    unnamed x28 -> x21, local copies, waits for them, and re-layouts: 0.61 us -> 5.01 us
    another operation x2 -> x0, other arithmetic: 1.74 us -> none
    unnamed x2 -> x0, other arithmetic: 1.32 us -> none
    reduce_sum x1 -> x0, other arithmetic: 1 us -> none  [on_device(): step = mine - step_size * sums.astype(f32).sum(0)]
    transpose x1, local copies, waits for them, and re-layouts: 0.09 us -> 1.07 us  [banded(): small = jnp.transpose(kernel, order).reshape(taps * 3 * outs, units * ins)]
    sub x1 -> x0, other arithmetic: 0.86 us -> none  [on_device(): step = mine - step_size * sums.astype(f32).sum(0)]
where the time goes in v2:
time: 61.3 us; the launch traced here: 61 us
  Pallas kernels  48.3 us (79%)
  local copies, waits for them, and re-layouts  7.92 us (13%)
  other arithmetic  2.83 us (5%)
  matrix products  1.16 us (2%)
  between operations  0.83 us (1%)
    pallas_call x1, Pallas kernels, on_device(): pl.pallas_call(step_kernel, out_shape=[jax.ShapeDtypeStruct(iterate.shape...  48.3 us
    unnamed x21, local copies, waits for them, and re-layouts  5.01 us
    reduce_sum x3, other arithmetic, banded(): return chosen.sum(2).astype(bf16).reshape(taps, slices * outs, -1)  2.83 us
    convert_element_type x4, local copies, waits for them, and re-layouts, banded(): return chosen.sum(2).astype(bf16).reshape(taps, slices * outs, -1)  1.51 us

profile of v2, /device:TPU:0, one launch (start us, length us, event | category | flops | bytes accessed | tf_op | source)
XLA Modules:
  0.0 61.0 jit_solution(11531308483330910140)
XLA Ops:
  0.6 0.0 copy-start.1
  0.6 0.0 copy-start
  0.7 1.1 %copy.49 = bf16[3,3,24,3,24]{4,3,2,1,0:T(4,128)(2,1)S(1)} copy(bf16[3,3,24,3,24]{4,2,3,0,1:T(8,128)(2,1)} %bitcast.51) | data formatting | bytes 62208 | tf_op jit(solution)/shard_map/transpose | solution.py:156
  1.7 0.1 reshape.133
  1.9 0.0 copy-done.1
  1.9 0.2 convolution_bitcast_fusion.1
  2.1 0.0 copy-done
  2.1 0.0 copy-start.3
  2.2 0.3 convolution_bitcast_fusion
  2.5 0.5 copy-done.3
  3.0 0.0 copy-start.4
  3.0 0.0 copy-start.6
  3.0 0.0 copy-start.2
  3.0 0.0 copy-start.8
  3.0 2.0 %multiply_reduce_fusion = (bf16[3,8,24,576]{3,2,1,0:T(8,128)(2,1)}, bf16[3,8,24,576]{3,2,1,0:T(8,128)(2,1)}) fusion(f32[3,3,24,576]{3,2,1,0:T(8,128)S(1)} %convolution_bitcast_fusion, f32[8,3,576]{2,1,0:T(4,128)S(1)} %copy-done.3, f32[3,3,24,576]{3,2,1,0:T(8,128)S(1)} %convolution_bitcast_fusion.1), kind=kLoop, calls=%fused_computation | loop fusion | flops 3317760 | bytes 2377728 | tf_op jit(solution)/shard_map/reduce_sum | solution.py:165
  5.0 0.0 copy-done.4
  5.0 0.0 copy-done.6
  5.0 0.0 copy-start.5
  5.1 0.1 convolution_bitcast_fusion.2
  5.2 0.0 copy-start.7
  5.2 0.0 copy-done.2
  5.3 0.1 convolution_bitcast_fusion.3
  5.4 0.0 copy-done.8
  5.4 0.1 multiply_reduce_fusion.4
  5.5 0.1 copy.52
  5.6 0.7 %convert_element_type.111.rest_10_ = bf16[9,16,192]{2,1,0:T(8,128)(2,1)} reshape(bf16[9,8,2,192]{3,2,1,0:T(2,128)(2,1)S(1)} %copy.52) | data formatting | bytes 110592 | tf_op jit(solution)/shard_map/convert_element_type | solution.py:165
  6.3 0.1 copy.55
  6.3 0.7 %convert_element_type.113.rest_11_ = bf16[9,16,192]{2,1,0:T(8,128)(2,1)} reshape(bf16[9,8,2,192]{3,2,1,0:T(2,128)(2,1)S(1)} %copy.55) | data formatting | bytes 110592 | tf_op jit(solution)/shard_map/convert_element_type | solution.py:165
  7.1 0.0 copy-done.5
  7.1 0.2 convolution_bitcast_fusion.4
  7.3 0.2 convolution_bitcast_fusion.5
  7.5 0.0 copy-done.7
  7.5 0.8 %multiply_reduce_fusion.2 = (bf16[8,24,144]{2,1,0:T(8,128)(2,1)}, bf16[8,24,144]{2,1,0:T(8,128)(2,1)}) fusion(f32[3,24,144]{2,1,0:T(8,128)S(1)} %convolution_bitcast_fusion.4, f32[8,3,144]{2,1,0:T(4,128)S(1)} %copy-done.7, f32[3,24,144]{2,1,0:T(8,128)S(1)} %convolution_bitcast_fusion.5), kind=kLoop, calls=%fused_computation.8 | loop fusion | flops 276480 | bytes 207360 | tf_op jit(solution)/shard_map/reduce_sum | solution.py:165
  8.3 48.3 %shard_map.301 = (f32[2,1,64,128]{3,2,1,0:T(8,128)}, f32[2,1,64,128]{3,2,1,0:T(8,128)}, f32[2,1,64,128]{3,2,1,0:T(8,128)}) custom-call(f32[2,2,1,256,128]{4,3,2,1,0:T(8,128)} %maps.1, f32[2,2,1,256,128]{4,3,2,1,0:T(8,128)} %kspace.1, s32[256,128]{1,0:T(8,128)} %mask.1, f32[2,1,64,128]{3,2,1,0:T(8,128)} %iterate.1, s32[2,1,64,128]{3,2,1,0:T(8,128)} %probe_bits.1, ...), custom_call_target="tpu_custom_call" | custom-call | tf_op jit(solution)/shard_map/pallas_call | solution.py:408
  56.6 1.5 %copy.73 = f32[2,1,64,128]{3,2,1,0:T(8,128)} copy(f32[2,1,64,128]{3,2,1,0:T(8,128)} %get-tuple-element.12) | data formatting | bytes 131072
  58.1 1.5 %copy.74 = f32[2,1,64,128]{3,2,1,0:T(8,128)} copy(f32[2,1,64,128]{3,2,1,0:T(8,128)} %get-tuple-element.13) | data formatting | bytes 131072
  59.5 1.5 %copy.75 = f32[2,1,64,128]{3,2,1,0:T(8,128)} copy(f32[2,1,64,128]{3,2,1,0:T(8,128)} %get-tuple-element.14) | data formatting | bytes 131072
  (7 shorter events, 0.2 us)
Async XLA Ops:
  0.6 1.2 %copy-start.1 = (bf16[72,576,1,1]{1,0,3,2:T(8,128)(2,1)S(1)}, bf16[72,576,1,1]{1,0,3,2:T(8,128)(2,1)}, u32[]{:S(2)}) copy-start(bf16[72,576,1,1]{1,0,3,2:T(8,128)(2,1)} %constant.55) | copy-start | bytes 248836
  0.6 1.5 %copy-start = (bf16[24,24,3,3,3]{1,0,4,3,2:T(8,128)(2,1)S(1)}, bf16[24,24,3,3,3]{1,0,4,3,2:T(8,128)(2,1)}, u32[]{:S(2)}) copy-start(bf16[24,24,3,3,3]{1,0,4,3,2:T(8,128)(2,1)} %param.38) | copy-start | bytes 93316
  2.1 0.9 %copy-start.3 = (f32[8,3,576]{2,1,0:T(4,128)S(1)}, f32[8,3,576]{2,1,0:T(4,128)}, u32[]{:S(2)}) copy-start(f32[8,3,576]{2,1,0:T(4,128)} %constant.29.clone) | copy-start | bytes 165892
  3.0 2.0 %copy-start.4 = (bf16[24,2,3,3,3]{0,1,4,3,2:T(2,128)(2,1)S(1)}, bf16[24,2,3,3,3]{0,1,4,3,2:T(2,128)(2,1)}, u32[]{:S(2)}) copy-start(bf16[24,2,3,3,3]{0,1,4,3,2:T(2,128)(2,1)} %param.37) | copy-start | bytes 7780
  3.0 2.0 %copy-start.6 = (bf16[24,192,1,1]{1,0,3,2:T(8,128)(2,1)S(1)}, bf16[24,192,1,1]{1,0,3,2:T(8,128)(2,1)}, u32[]{:S(2)}) copy-start(bf16[24,192,1,1]{1,0,3,2:T(8,128)(2,1)} %constant.56) | copy-start | bytes 27652
  3.0 2.2 %copy-start.2 = (bf16[2,24,3,3,3]{1,0,4,3,2:T(2,128)(2,1)S(1)}, bf16[2,24,3,3,3]{1,0,4,3,2:T(2,128)(2,1)}, u32[]{:S(2)}) copy-start(bf16[2,24,3,3,3]{1,0,4,3,2:T(2,128)(2,1)} %param.39) | copy-start | bytes 7780
  3.0 2.4 %copy-start.8 = (f32[8,3,192]{2,0,1:T(8,128)S(1)}, f32[8,3,192]{2,0,1:T(8,128)}, u32[]{:S(2)}) copy-start(f32[8,3,192]{2,0,1:T(8,128)} %constant.31.clone) | copy-start | bytes 55300
  5.0 2.1 %copy-start.5 = (bf16[18,144,1]{1,0,2:T(8,128)(2,1)S(1)}, bf16[18,144,1]{1,0,2:T(8,128)(2,1)}, u32[]{:S(2)}) copy-start(bf16[18,144,1]{1,0,2:T(8,128)(2,1)} %constant.54) | copy-start | bytes 15556
  5.2 2.3 %copy-start.7 = (f32[8,3,144]{2,1,0:T(4,128)S(1)}, f32[8,3,144]{2,1,0:T(4,128)}, u32[]{:S(2)}) copy-start(f32[8,3,144]{2,1,0:T(4,128)} %constant.27.clone) | copy-start | bytes 41476

commit v3 on v2

--- a/solution.py
+++ b/solution.py
@@ -149,20 +149,57 @@
     )
 
 
-def banded(kernel, slices, form):
+forms = {"in": ((2, 0, 3, 4, 1), 1, 9), "mid": ((3, 2, 0, 4, 1), 3, 3), "out": ((3, 4, 2, 0, 1), 9, 1)}
+
+
+def small_kernel(kernel, form):
+    order, taps, units = forms[form]
     outs, ins = kernel.shape[:2]
-    order = {"in": (2, 0, 3, 4, 1), "mid": (3, 2, 0, 4, 1), "out": (3, 4, 2, 0, 1)}[form]
-    taps, units = {"in": (1, 9), "mid": (3, 3), "out": (9, 1)}[form]
-    small = jnp.transpose(kernel, order).reshape(taps * 3 * outs, units * ins)
-    spread = np.kron(np.eye(units), np.tile(np.eye(ins), (1, slices)))
-    wide = dot(small, jnp.asarray(spread, bf16)).reshape(taps, 1, 3, outs, -1)
-    lane_slice = np.tile(np.repeat(np.arange(slices), ins), units)
-    inside = (
-        lane_slice[None, None, :]
-        == (np.arange(slices)[:, None, None] + np.arange(3)[None, :, None] - 1)
-    )
-    chosen = wide * jnp.asarray(inside, f32)[None, :, :, None, :]
-    return chosen.sum(2).astype(bf16).reshape(taps, slices * outs, -1)
+    return jnp.transpose(kernel, order).reshape(taps * 3 * outs, units * ins)
+
+
+def band_constants(kernel, slices, form):
+    _, taps, units = forms[form]
+    outs, ins = kernel.shape[:2]
+    spread = jnp.asarray(np.kron(np.eye(units), np.tile(np.eye(ins), (1, slices))), bf16)
+    lanes = np.tile(np.repeat(np.arange(slices), ins), units)
+    if form != "out":
+        return spread, jnp.asarray(lanes[None, :], f32)
+    row_slices = np.repeat(np.arange(slices), outs)
+    bands = np.stack([lanes[None, :] == row_slices[:, None] + dx - 1 for dx in range(3)])
+    repeat = np.stack(
+        [
+            np.kron(np.eye(taps), np.tile(np.eye(3 * outs)[dx * outs : (dx + 1) * outs], (slices, 1)))
+            for dx in range(3)
+        ]
+    )
+    return spread, jnp.asarray(bands, f32), jnp.asarray(repeat, bf16)
+
+
+def build_rows(small, spread, lanes, target):
+    taps, inner = target.shape[:2]
+    outs = small.shape[0] // (3 * taps)
+    wide = dot(small[...], spread[...])
+    lane_slice = lanes[...]
+    for tap in range(taps):
+        blocks = []
+        for out_slice in range(inner // outs):
+            block = None
+            for dx in range(3):
+                at = (tap * 3 + dx) * outs
+                term = jnp.where(lane_slice == float(out_slice + dx - 1), wide[at : at + outs], 0.0)
+                block = term if block is None else block + term
+            blocks.append(block)
+        target[tap] = jnp.concatenate(blocks, axis=0).astype(bf16)
+
+
+def build_taps(small, spread, bands, repeat, target):
+    wide = dot(small[...], spread[...]).astype(bf16)
+    total = None
+    for dx in range(3):
+        term = dot(repeat[dx], wide).reshape(target.shape) * bands[dx][None]
+        total = term if total is None else total + term
+    target[...] = total.astype(bf16)
 
 
 def transposed(kernel):
@@ -219,13 +256,14 @@
     return total
 
 
-def step_kernel(maps, kspace, mask, iterate, probe_bits, loss_gradient, adjoint, *rest):
-    tables, weights, rest = rest[:8], rest[8:14], rest[14:]
+def step_kernel(maps, kspace, mask, iterate, probe_bits, adjoint, *rest):
+    tables, smalls, bands, rest = rest[:8], rest[8:14], rest[14:21], rest[21:]
+    in_band, mid_band, out_band = bands[:2], bands[2:4], bands[4:]
+    changes = rest[0]
+    (padded, work, rows_work, own_iterate, own_fields, all_iterate, all_fields, parts_send, parts,
+     fields_send, fields, delta_send, delta, pulled_send, pulled, sums_send, sums, *weights) = rest[1:24]
     first, second, last, first_t, second_t, last_t = weights
-    new_out, probe_out, adjoint_out = rest[:3]
-    (padded, work, rows_work, own_iterate, own_fields, all_iterate, all_fields, parts_send, parts,
-     fields_send, fields, delta_send, delta, pulled_send, pulled, sums_send, sums) = rest[3:20]
-    sems = rest[20:]
+    sems = rest[24:]
     channels = []
     for index, (axes, how, source, target) in enumerate((
         (("coil",), "all", own_iterate, all_iterate),
@@ -305,6 +343,12 @@
             rows_work[:, row, :] = values[:, row * depth : (row + 1) * depth]
         return rows_work[...].reshape(slices, 2, own, depth)
 
+    build_rows(smalls[5], *in_band, last_t)
+    build_rows(smalls[0], *in_band, first)
+    build_rows(smalls[1], *mid_band, second)
+    build_rows(smalls[4], *mid_band, second_t)
+    build_taps(smalls[2], *out_band, last)
+    build_taps(smalls[3], *out_band, first_t)
     window_way.finish()
     started = load(fields[:, 0:2].astype(f32))
     grads = []
@@ -350,9 +394,8 @@
     for part in range(2):
         for piece in range(slices):
             at = piece * own
-            new_out[part, 0, at : at + own] = iterate[part, 0, at : at + own] + delta[piece, part]
-    starts = (sign, loss_gradient[...] + adjoint[...])
-    for field, out in ((0, probe_out), (1, adjoint_out)):
+            changes[0, part, at : at + own] = delta[piece, part]
+    for field in range(2):
         sum_ways[field].finish()
         for part in range(2):
             added = sums[field, 0, part].astype(f32)
@@ -365,7 +408,7 @@
                 ],
                 axis=0,
             )
-            out[part, 0] = starts[field][part, 0] + (mine - step_size * added)
+            changes[1 + field, part] = mine - step_size * added
 
 
 def on_device(coil_maps, kspace, sample_mask, iterate, probe_bits, loss_gradient, adjoint,
@@ -377,14 +420,17 @@
     window = own + 2 * reach
     rows = iterate.shape[2]
     tables = fourier_tables(height, depth, -1.0) + fourier_tables(height, depth, 1.0)
-    forward = [
-        banded(kernel, slabs, form)
-        for kernel, form in ((kernel_first, "in"), (kernel_second, "mid"), (kernel_last, "out"))
+    kernels = (kernel_first, kernel_second, kernel_last)
+    smalls = [small_kernel(kernel, form) for kernel, form in zip(kernels, ("in", "mid", "out"))]
+    smalls += [
+        small_kernel(transposed(kernel), form) for kernel, form in zip(kernels, ("out", "mid", "in"))
     ]
-    backward = [
-        banded(transposed(kernel), slabs, form)
-        for kernel, form in ((kernel_first, "out"), (kernel_second, "mid"), (kernel_last, "in"))
+    constants = [
+        constant
+        for kernel, form in zip(kernels, ("in", "mid", "out"))
+        for constant in band_constants(kernel, slabs, form)
     ]
+    hidden, channels = kernel_second.shape[0] * slabs, kernel_first.shape[1] * slabs
     buffers = [
         ((6, height + 2 * reach + 8, depth), f32),
         ((2 * slabs, window, depth), f32),
@@ -403,18 +449,26 @@
         ((2, pieces, 2, own, depth), bf16),
         ((2, coils, 2, rows, depth), bf16),
         ((2, coils, 2, rows, depth), bf16),
+        ((1, hidden, 9 * channels), bf16),
+        ((3, hidden, 3 * hidden), bf16),
+        ((9, channels, hidden), bf16),
+        ((9, channels, hidden), bf16),
+        ((3, hidden, 3 * hidden), bf16),
+        ((1, hidden, 9 * channels), bf16),
     ]
     ways = (coils, coils, slabs, pieces, slabs, pieces, pieces, coils, coils)
-    return pl.pallas_call(
+    changes = pl.pallas_call(
         step_kernel,
-        out_shape=[jax.ShapeDtypeStruct(iterate.shape, f32)] * 3,
-        in_specs=[vmem] * 21,
-        out_specs=[vmem] * 3,
+        out_shape=jax.ShapeDtypeStruct((3, 2, rows, depth), f32),
+        in_specs=[vmem] * 27,
+        out_specs=vmem,
         scratch_shapes=[pltpu.VMEM(shape, kind) for shape, kind in buffers]
         + [pltpu.SemaphoreType.DMA((size,)) for size in ways for _ in range(2)],
         compiler_params=pltpu.CompilerParams(collective_id=0, has_side_effects=True),
-    )(coil_maps, kspace, sample_mask, iterate, probe_bits, loss_gradient, adjoint,
-      *tables, *forward, *backward)
+    )(coil_maps, kspace, sample_mask, iterate, probe_bits, adjoint, *tables, *smalls, *constants)
+    changes = changes[:, :, None]
+    sign = (2 * probe_bits - 1).astype(f32)
+    return iterate + changes[0], sign + changes[1], loss_gradient + (adjoint + changes[2])
 
 
 def solution(mesh):

time: 61.3 us -> 56.4 us (0.920)
  local copies, waits for them, and re-layouts: 7.92 us -> 5.82 us
  other arithmetic: 2.83 us -> 1.59 us
  matrix products: 1.16 us -> 0 us
    unnamed x21 -> x14, local copies, waits for them, and re-layouts: 5.01 us -> 0.16 us
    reshape x0 -> x10, local copies, waits for them, and re-layouts: none -> 4.66 us  [small_kernel(): return jnp.transpose(kernel, order).reshape(taps * 3 * outs, units * ins)]
    reduce_sum x3 -> x0, other arithmetic: 2.83 us -> none  [banded(): return chosen.sum(2).astype(bf16).reshape(taps, slices * outs, -1)]
    unnamed x0 -> x1, other arithmetic: none -> 1.59 us
    convert_element_type x4 -> x0, local copies, waits for them, and re-layouts: 1.51 us -> none  [banded(): return chosen.sum(2).astype(bf16).reshape(taps, slices * outs, -1)]
    dot_general x6 -> x0, matrix products: 1.16 us -> none  [dot(): return jnp.dot(left, right, preferred_element_type=f32)]
    transpose x1 -> x2, local copies, waits for them, and re-layouts: 1.07 us -> 0.02 us  [small_kernel(): return jnp.transpose(kernel, order).reshape(taps * 3 * outs, units * ins)]
    another operation x4 -> x5, local copies, waits for them, and re-layouts: 0.21 us -> 0.98 us  [small_kernel(): return jnp.transpose(kernel, order).reshape(taps * 3 * outs, units * ins)]
where the time goes in v3:
time: 56.4 us; the launch traced here: 56.1 us
  Pallas kernels  47.9 us (85%)
  local copies, waits for them, and re-layouts  5.82 us (10%)
  other arithmetic  1.59 us (3%)
  between operations  0.74 us (1%)
    pallas_call x1, Pallas kernels, on_device(): pl.pallas_call(step_kernel, out_shape=jax.ShapeDtypeStruct((3, 2, rows, d...  47.9 us
    reshape x10, local copies, waits for them, and re-layouts, small_kernel(): return jnp.transpose(kernel, order).reshape(taps * 3 * outs, units * ins)  4.66 us
    unnamed x1, other arithmetic  1.59 us

profile of v3, /device:TPU:0, one launch (start us, length us, event | category | flops | bytes accessed | tf_op | source)
XLA Modules:
  0.0 56.1 jit_solution(12627483207706502859)
XLA Ops:
  0.6 0.9 %reverse_bitcast_fusion = bf16[3,3,24,3,24]{2,4,3,0,1:T(8,128)(2,1)S(1)} fusion(bf16[24,24,3,3,3]{1,0,4,3,2:T(8,128)(2,1)} %param.33), kind=kLoop, calls=%fused_computation | loop fusion | bytes 62208 | tf_op jit(solution)/shard_map/transpose;transpose | solution.py:158
  1.6 0.2 copy.59
  1.7 0.0 copy-start
  1.8 0.8 %reshape.37.rest_12_ = bf16[216,72]{1,0:T(8,128)(2,1)} reshape(bf16[3,3,24,3,24]{4,3,2,1,0:T(4,128)(2,1)S(1)} %copy.59) | data formatting | bytes 62208 | tf_op jit(solution)/shard_map/reshape | solution.py:158
  2.5 0.1 copy-done
  2.7 0.1 copy.58
  2.8 0.0 copy-start.5
  2.8 0.8 %reshape.36.rest_9_ = bf16[216,72]{1,0:T(8,128)(2,1)} reshape(bf16[3,3,24,3,24]{4,3,2,1,0:T(4,128)(2,1)S(1)} %copy.58) | data formatting | bytes 62208 | tf_op jit(solution)/shard_map/reshape | solution.py:158
  3.5 0.0 copy-done.5
  3.6 0.1 reshape.35
  3.7 0.0 copy-start.6
  3.7 0.7 %copy.50.rest_13_ = bf16[72,18]{1,0:T(8,128)(2,1)} copy(bf16[72,18]{0,1:T(8,128)(2,1)S(1)} %reshape.35) | data formatting | bytes 5184 | tf_op jit(solution)/shard_map/reshape | solution.py:158
  4.4 0.0 copy-done.6
  4.4 0.1 reshape.30
  4.5 0.7 %copy.47.rest_8_ = bf16[72,18]{1,0:T(8,128)(2,1)} copy(bf16[72,18]{0,1:T(8,128)(2,1)S(1)} %reshape.30) | data formatting | bytes 5184 | tf_op jit(solution)/shard_map/reshape | solution.py:158
  5.2 0.6 %reshape.33.rest_11_ = bf16[54,24]{1,0:T(8,128)(2,1)} reshape(bf16[3,3,3,2,24]{4,3,2,1,0:T(2,128)(2,1)S(1)} %copy.44) | data formatting | bytes 5184 | tf_op jit(solution)/shard_map/reshape | solution.py:158
  5.9 0.6 %reshape.32.rest_10_ = bf16[54,24]{1,0:T(8,128)(2,1)} reshape(bf16[3,3,3,2,24]{4,3,2,1,0:T(2,128)(2,1)S(1)} %copy.43) | data formatting | bytes 5184 | tf_op jit(solution)/shard_map/reshape | solution.py:158
  6.5 0.0 copy-start.1
  6.5 0.0 copy-start.2
  6.5 0.0 copy-start.3
  6.5 0.0 copy-start.4
  6.5 47.9 %shard_map.256 = f32[3,2,64,128]{3,2,1,0:T(8,128)} custom-call(f32[2,2,1,256,128]{4,3,2,1,0:T(8,128)} %maps.1, f32[2,2,1,256,128]{4,3,2,1,0:T(8,128)} %kspace.1, s32[256,128]{1,0:T(8,128)} %mask.1, f32[2,1,64,128]{3,2,1,0:T(8,128)} %iterate.1, s32[2,1,64,128]{3,2,1,0:T(8,128)} %probe_bits.1, f32[2,1,64,128]{3,2,1,0:T(8,128)} %adjoint.1, ...), custom_call_target="tpu_custom_call" | custom-call | tf_op jit(solution)/shard_map/pallas_call | solution.py:460
  54.5 0.0 copy-done.1
  54.5 0.0 copy-done.2
  54.5 0.0 copy-done.3
  54.5 0.0 copy-done.4
  54.5 1.6 %fusion.1 = (f32[2,1,64,128]{3,2,1,0:T(8,128)}, f32[2,1,64,128]{3,2,1,0:T(8,128)}, f32[2,1,64,128]{3,2,1,0:T(8,128)}) fusion(f32[2,1,64,128]{3,2,1,0:T(8,128)S(1)} %copy-done.1, f32[2,1,64,128]{3,2,1,0:T(8,128)S(1)} %copy-done.4, f32[3,2,64,128]{3,2,1,0:T(8,128)} %shard_map.256, s32[2,1,64,128]{3,2,1,0:T(8,128)S(1)} %copy-done.3, ...), kind=kLoop, calls=%fused_computation.3 | loop fusion | flops 114688 | bytes 655360
  (6 shorter events, 0.1 us)
Async XLA Ops:
  1.7 0.9 %copy-start = (bf16[24,24,3,3,3]{1,0,4,3,2:T(8,128)(2,1)S(1)}, bf16[24,24,3,3,3]{1,0,4,3,2:T(8,128)(2,1)}, u32[]{:S(2)}) copy-start(bf16[24,24,3,3,3]{1,0,4,3,2:T(8,128)(2,1)} %param.33) | copy-start | bytes 93316
  2.8 0.8 %copy-start.5 = (bf16[2,24,3,3,3]{1,0,4,3,2:T(2,128)(2,1)S(1)}, bf16[2,24,3,3,3]{1,0,4,3,2:T(2,128)(2,1)}, u32[]{:S(2)}) copy-start(bf16[2,24,3,3,3]{1,0,4,3,2:T(2,128)(2,1)} %param.34) | copy-start | bytes 7780
  3.7 0.7 %copy-start.6 = (bf16[24,2,3,3,3]{0,1,4,3,2:T(2,128)(2,1)S(1)}, bf16[24,2,3,3,3]{0,1,4,3,2:T(2,128)(2,1)}, u32[]{:S(2)}) copy-start(bf16[24,2,3,3,3]{0,1,4,3,2:T(2,128)(2,1)} %param.32) | copy-start | bytes 7780
  6.5 48.0 %copy-start.1 = (f32[2,1,64,128]{3,2,1,0:T(8,128)S(1)}, f32[2,1,64,128]{3,2,1,0:T(8,128)}, u32[]{:S(2)}) copy-start(f32[2,1,64,128]{3,2,1,0:T(8,128)} %adjoint.1) | copy-start | bytes 196612
  6.5 48.0 %copy-start.2 = (f32[2,1,64,128]{3,2,1,0:T(8,128)S(1)}, f32[2,1,64,128]{3,2,1,0:T(8,128)}, u32[]{:S(2)}) copy-start(f32[2,1,64,128]{3,2,1,0:T(8,128)} %iterate.1) | copy-start | bytes 196612
  6.5 48.0 %copy-start.3 = (s32[2,1,64,128]{3,2,1,0:T(8,128)S(1)}, s32[2,1,64,128]{3,2,1,0:T(8,128)}, u32[]{:S(2)}) copy-start(s32[2,1,64,128]{3,2,1,0:T(8,128)} %probe_bits.1) | copy-start | bytes 196612
  6.5 48.0 %copy-start.4 = (f32[2,1,64,128]{3,2,1,0:T(8,128)S(1)}, f32[2,1,64,128]{3,2,1,0:T(8,128)}, u32[]{:S(2)}) copy-start(f32[2,1,64,128]{3,2,1,0:T(8,128)} %param.30) | copy-start | bytes 196612
